TPU v7x, 32 devices: a whole 2x2x4 slice. The times are simulated.
32 devices in a mesh: seq: 16 (over z, y, x), tp: 2 (over core).
Axes of the slice: x: 2, y: 2, z: 4, core: 2. Of those that a mesh axis runs over, the one named last changes fastest.
Arguments:
- queries: bfloat16 [8192, 4096], P('seq', 'tp'), may hold values from -9 to 9
- keys: bfloat16 [8192, 4096], P('seq', 'tp'), may hold values from -9 to 9
- values: bfloat16 [8192, 4096], P('seq', 'tp'), may hold values from -6 to 6
- route: int32 [32, 8192], P('tp', 'seq'), may hold values from 0 to 8191, as said below
- members: int32 [32, 8192], P('tp', 'seq'), may hold values from 0 to 8191, as said below
- pattern: int32 [32, 32, 10], P('tp', 'seq'), may hold values from 0 to 1, as said below
- w_out: bfloat16 [4096, 4096], P('tp', 'seq'), may hold values from -0.125 to 0.125
Outputs:
- mixed: bfloat16 [8192, 4096], P('seq', 'tp')
Inputs may be any that keep to these rules, and one draw needn't show every extreme that they name: `route`: each row is a permutation of the positions; for every aligned block of 512 positions and every aligned block of 512 slots, exactly 32 of the block's positions have their slot in that slot block. members[h] is the inverse permutation of route[h]: members[h, route[h, p]] = p. `pattern`: entries 2 * 2 and 2 * 2 + 1 (the cluster's own blocks) are always 1; entries whose cluster lies outside 0 to 31 are always 0.
All inputs are finite; a program needn't handle non-finite values.
Results may differ from a plain program's by a relative error of at most 0.017.
Values may be sent and summed in bfloat16 or wider, within the bound.
No kernel may reach another device: no remote copies, remote signals or barrier semaphores. Data moves between devices by JAX's collectives and lax.ppermute only.
A program may use at most 128 MiB of HBM per device.

v0:
```python
import jax
import jax.numpy as jnp
from jax import lax
from jax.sharding import PartitionSpec as P

CLUSTER = 256
REACH = 2


def extended_2(cells, sides, width):
    for axis, dim in sides:
        count = lax.axis_size(axis)
        ends = count - 1
        head = lax.slice_in_dim(cells, 0, width, axis=dim)
        tail = lax.slice_in_dim(cells, cells.shape[dim] - width, cells.shape[dim], axis=dim)
        cells = jnp.concatenate(
            [
                lax.ppermute(tail, axis, [(i, (i + 1) % count) for i in range(ends)]),
                cells,
                lax.ppermute(head, axis, [((i + 1) % count, i) for i in range(ends)]),
            ],
            axis=dim,
        )
    return cells


def attend_head(pieces):
    query_rows, key_rows, value_rows, pattern_rows = pieces
    head_width = query_rows.shape[1]
    cluster_count = query_rows.shape[0] // CLUSTER
    window_rows = (2 * REACH + 1) * CLUSTER
    starts = jnp.arange(cluster_count) * CLUSTER
    key_window = jax.vmap(
        lambda slot_start: lax.dynamic_slice_in_dim(key_rows, slot_start, window_rows, 0)
    )(starts)
    value_window = jax.vmap(
        lambda slot_start: lax.dynamic_slice_in_dim(value_rows, slot_start, window_rows, 0)
    )(starts)
    query_blocks = query_rows.reshape(cluster_count, CLUSTER, head_width)
    scores = jnp.einsum(
        "cqd,ckd->cqk", query_blocks, key_window, preferred_element_type=jnp.float32
    ) * head_width ** (-0.5)
    allowed = jnp.repeat(pattern_rows, CLUSTER // 2, axis=1) > 0
    scores = jnp.where(allowed[:, None, :], scores, -jnp.inf)
    row_max = jnp.max(scores, axis=-1, keepdims=True)
    exponent = jnp.exp(scores - row_max)
    weights = (exponent / jnp.sum(exponent, axis=-1, keepdims=True)).astype(jnp.bfloat16)
    context = jnp.einsum(
        "cqk,ckd->cqd", weights, value_window, preferred_element_type=jnp.float32
    ).astype(jnp.bfloat16)
    return context.reshape(query_rows.shape[0], head_width)


def buffer_index(group_of, order_key, per_peer):
    same_group = group_of[:, :, None] == group_of[:, None, :]
    earlier = order_key[:, None, :] < order_key[:, :, None]
    rank = jnp.sum((same_group & earlier).astype(jnp.int32), axis=2)
    return group_of * per_peer + rank


def shards(queries, keys, values, route, members, pattern, w_out):
    rows_here = queries.shape[0]
    head_count = route.shape[0]
    head_width = queries.shape[1] // head_count
    peer_count = lax.axis_size("seq")
    per_peer = rows_here // peer_count
    local_iota = jnp.arange(rows_here, dtype=jnp.int32)
    send_index = buffer_index(route // rows_here, route, per_peer)
    local_slots = jnp.broadcast_to(local_iota[None, :], members.shape)
    arrival_index = buffer_index(members // rows_here, local_slots, per_peer)
    send_table = (send_index[:, None, :] == local_iota[None, :, None]).astype(jnp.bfloat16)
    land_table = (arrival_index[:, :, None] == local_iota[None, None, :]).astype(jnp.bfloat16)
    stacked = jnp.concatenate(
        [
            queries.reshape(rows_here, head_count, head_width),
            keys.reshape(rows_here, head_count, head_width),
            values.reshape(rows_here, head_count, head_width),
        ],
        axis=2,
    )
    packed = jnp.einsum(
        "hap,phd->had", send_table, stacked, preferred_element_type=jnp.float32
    ).astype(jnp.bfloat16)

    def outgoing(column_index):
        part_rows = packed[:, :, column_index * head_width : (column_index + 1) * head_width]
        return part_rows.reshape(head_count, peer_count, per_peer, head_width)

    sent_query, sent_key, sent_value = (
        lax.all_to_all(outgoing(0), "seq", split_axis=1, concat_axis=1, tiled=True),
        lax.all_to_all(outgoing(1), "seq", split_axis=1, concat_axis=1, tiled=True),
        lax.all_to_all(outgoing(2), "seq", split_axis=1, concat_axis=1, tiled=True),
    )
    arrived = jnp.concatenate(
        [
            sent_query.reshape(head_count, rows_here, head_width),
            sent_key.reshape(head_count, rows_here, head_width),
            sent_value.reshape(head_count, rows_here, head_width),
        ],
        axis=2,
    )
    placed = jnp.einsum(
        "hsa,had->hsd", land_table, arrived, preferred_element_type=jnp.float32
    ).astype(jnp.bfloat16)
    ordered_query = placed[:, :, :head_width]
    keys_values = jnp.stack(
        [placed[:, :, head_width : 2 * head_width], placed[:, :, 2 * head_width :]]
    )
    extended = extended_2(keys_values, (("seq", 2),), REACH * CLUSTER)
    context = lax.map(attend_head, (ordered_query, extended[0], extended[1], pattern))
    returning = jnp.einsum(
        "hsa,hsd->had", land_table, context, preferred_element_type=jnp.float32
    ).astype(jnp.bfloat16)
    returning = returning.reshape(head_count, peer_count, per_peer, head_width)
    returned = lax.all_to_all(returning, "seq", split_axis=1, concat_axis=1, tiled=True).reshape(
        head_count, rows_here, head_width
    )
    attended = jnp.einsum(
        "hap,had->phd", send_table, returned, preferred_element_type=jnp.float32
    ).astype(jnp.bfloat16)
    attended = attended.reshape(rows_here, head_count * head_width)
    partial_value = jnp.dot(
        attended,
        lax.all_gather(w_out, "seq", axis=1, tiled=True),
        preferred_element_type=jnp.float32,
    )
    mixed_out = lax.psum_scatter(
        partial_value.astype(jnp.bfloat16), "tp", scatter_dimension=1, tiled=True
    )
    return mixed_out


def solution(mesh):
    placed = (
        P("seq", "tp"),
        P("seq", "tp"),
        P("seq", "tp"),
        P("tp", "seq"),
        P("tp", "seq"),
        P("tp", "seq", None),
        P("tp", "seq"),
    )
    return jax.shard_map(
        shards, mesh=mesh, in_specs=placed, out_specs=P("seq", "tp"), check_vma=False
    )
```

profile of v0, /device:TPU:0, one launch (start us, length us, event | category | flops | bytes accessed | tf_op | source)
XLA Modules:
  0.0 651.4 jit_solution(5941121818779080078)
XLA Ops:
  7.3 5.3 convert_reduce_fusion
  13.4 2.9 copy.37
  18.7 2.9 copy.38
  21.5 2.4 copy.41
  23.9 2.9 copy.39
  26.8 2.4 copy.42
  29.2 6.6 %fusion.34 = bf16[16,512,384]{2,1,0:T(8,128)(2,1)S(1)} fusion(bf16[512,16,128]{2,0,1:T(8,128)(2,1)} %copy.42, bf16[512,16,128]{2,0,1:T(8,128)(2,1)} %copy.41, bf16[512,16,128]{2,0,1:T(8,128)(2,1)} %copy.40, s32[16,512]{1,0:T(8,128)S(1)} %multiply_add_fusion), kind=kOutput, calls=%fused_computation.54 | convolution fusion | flops 3247439872 | bytes 12615680 | tf_op jit(solution)/shard_map/hap,phd->had/dot_general | solution.py:81
  35.8 3.8 fusion.46
  41.5 8.3 %all-to-all-start.1 = ((bf16[16,16,32,128]{3,2,0,1:T(8,128)(2,1)}), bf16[16,16,32,128]{3,2,0,1:T(8,128)(2,1)S(1)}, u32[]{:S(2)}, u32[]{:S(2)}) async-start(bf16[16,16,32,128]{3,2,0,1:T(8,128)(2,1)} %copy.45), calls=%async_computation.1 | async-start | bytes 4194304 | tf_op jit(solution)/shard_map/all_to_all | solution.py:91
  49.8 3.4 copy.47
  53.3 39.6 %all-to-all-done.1 = bf16[16,16,32,128]{3,2,0,1:T(8,128)(2,1)S(1)} async-done(((bf16[16,16,32,128]{3,2,0,1:T(8,128)(2,1)}), bf16[16,16,32,128]{3,2,0,1:T(8,128)(2,1)S(1)}, u32[]{:S(2)}, u32[]{:S(2)}) %all-to-all-start.1) | async-done | bytes 2097184 | tf_op jit(solution)/shard_map/all_to_all | solution.py:91
  92.9 10.1 %all-to-all-start.2 = ((bf16[16,16,32,128]{3,2,0,1:T(8,128)(2,1)}), bf16[16,16,32,128]{3,2,0,1:T(8,128)(2,1)}, u32[]{:S(2)}, u32[]{:S(2)}) async-start(bf16[16,16,32,128]{3,2,0,1:T(8,128)(2,1)} %copy.47), calls=%async_computation.2 | async-start | bytes 4194304 | tf_op jit(solution)/shard_map/all_to_all | solution.py:92
  102.9 3.5 copy.43
  106.4 39.1 %all-to-all-done.2 = bf16[16,16,32,128]{3,2,0,1:T(8,128)(2,1)} async-done(((bf16[16,16,32,128]{3,2,0,1:T(8,128)(2,1)}), bf16[16,16,32,128]{3,2,0,1:T(8,128)(2,1)}, u32[]{:S(2)}, u32[]{:S(2)}) %all-to-all-start.2) | async-done | bytes 2097184 | tf_op jit(solution)/shard_map/all_to_all | solution.py:92
  145.5 9.9 %all-to-all-start = ((bf16[16,16,32,128]{3,2,0,1:T(8,128)(2,1)}), bf16[16,16,32,128]{3,2,0,1:T(8,128)(2,1)}, u32[]{:S(2)}, u32[]{:S(2)}) async-start(bf16[16,16,32,128]{3,2,0,1:T(8,128)(2,1)} %copy.43), calls=%async_computation | async-start | bytes 4194304 | tf_op jit(solution)/shard_map/all_to_all | solution.py:90
  155.7 4.3 convert_reduce_fusion.1
  161.9 3.6 copy.48
  165.6 32.4 %all-to-all-done = bf16[16,16,32,128]{3,2,0,1:T(8,128)(2,1)} async-done(((bf16[16,16,32,128]{3,2,0,1:T(8,128)(2,1)}), bf16[16,16,32,128]{3,2,0,1:T(8,128)(2,1)}, u32[]{:S(2)}, u32[]{:S(2)}) %all-to-all-start) | async-done | bytes 2097184 | tf_op jit(solution)/shard_map/all_to_all | solution.py:90
  200.3 4.8 fusion.31
  205.1 3.1 slice_bitcast_fusion.3
  208.3 2.5 pad_maximum_fusion.1
  210.9 4.9 collective-permute-start
  217.4 208.1 %collective-permute-done = bf16[2,16,512,128]{3,2,1,0:T(8,128)(2,1)} collective-permute-done((bf16[2,16,512,128]{3,2,1,0:T(8,128)(2,1)}, bf16[2,16,512,128]{3,2,1,0:T(8,128)(2,1)}, u32[]{:S(2)}, u32[]{:S(2)}) %collective-permute-start) | collective-permute-done | bytes 4194336 | tf_op jit(solution)/shard_map/ppermute | solution.py:18
  425.5 4.5 collective-permute-done.1
  430.0 6.5 pad_maximum_fusion
  436.5 5.6 slice_bitcast_fusion
  442.1 100.4 %while.16 = (s32[]{:T(128)}, bf16[16,512,128]{2,1,0:T(8,128)(2,1)}, s32[16,2,10]{2,1,0:T(2,128)S(1)}, bf16[16,512,128]{2,1,0:T(8,128)(2,1)}, bf16[16,1536,128]{2...) while((s32[]{:T(128)}, bf16[16,512,128]{2,1,0:T(8,128)(2,1)}, ...), condition=%wide.region_5.6_spmd, body=%wide.region_2.5_spmd.sunk | while | flops 509283360 | bytes 7096867 | solution.py:110
  542.5 4.3 fusion.37
  547.4 69.0 %all_to_all.20 = bf16[16,16,32,128]{3,2,0,1:T(8,128)(2,1)S(1)} all-to-all(bf16[16,16,32,128]{3,2,0,1:T(8,128)(2,1)S(1)} %copy.51), channel_id=1, replica_groups=mesh['seq'=16,'tp'=2] {'seq'}, dimensions={1} | all-to-all | bytes 4194304 | tf_op jit(solution)/shard_map/all_to_all | solution.py:115
  616.9 3.5 fusion.38
  620.4 14.0 %convolution_convert_fusion = bf16[512,4096]{1,0:T(8,128)(2,1)} fusion(bf16[512,2048]{0,1:T(8,128)(2,1)S(1)} %bitcast.106, bf16[2048,4096]{1,0:T(8,128)(2,1)} %all-gather.2.cloned.1.call-done), kind=kOutput, calls=%fused_computation.51 | convolution fusion | flops 8592031744 | bytes 23068672 | tf_op jit(solution)/shard_map/dot_general | solution.py:122
  634.4 10.2 %reduce-scatter.2.cloned.1.call-done = bf16[512,2048]{1,0:T(8,128)(2,1)} async-done(((bf16[512,4096]{1,0:T(8,128)(2,1)}), bf16[512,2048]{1,0:T(8,128)(2,1)}) %reduce-scatter.2.cloned.1.call-update) | async-done | bytes 2097168 | tf_op jit(solution)/shard_map/reduce_scatter | solution.py:127
  (381 shorter events, 123.4 us)
Async XLA Ops:
  41.5 51.4 %all-to-all-start.1 = ((bf16[16,16,32,128]{3,2,0,1:T(8,128)(2,1)}), bf16[16,16,32,128]{3,2,0,1:T(8,128)(2,1)S(1)}, u32[]{:S(2)}, u32[]{:S(2)}) async-start(bf16[16,16,32,128]{3,2,0,1:T(8,128)(2,1)} %copy.45), calls=%async_computation.1 | async-start | bytes 4194304 | tf_op jit(solution)/shard_map/all_to_all | solution.py:91
  92.9 52.6 %all-to-all-start.2 = ((bf16[16,16,32,128]{3,2,0,1:T(8,128)(2,1)}), bf16[16,16,32,128]{3,2,0,1:T(8,128)(2,1)}, u32[]{:S(2)}, u32[]{:S(2)}) async-start(bf16[16,16,32,128]{3,2,0,1:T(8,128)(2,1)} %copy.47), calls=%async_computation.2 | async-start | bytes 4194304 | tf_op jit(solution)/shard_map/all_to_all | solution.py:92
  102.9 52.7 %copy-start.3 = (s32[16,512]{1,0:T(8,128)S(1)}, s32[16,512]{1,0:T(8,128)}, u32[]{:S(2)}) copy-start(s32[16,512]{1,0:T(8,128)} %param.13) | copy-start | bytes 98308
  145.5 52.5 %all-to-all-start = ((bf16[16,16,32,128]{3,2,0,1:T(8,128)(2,1)}), bf16[16,16,32,128]{3,2,0,1:T(8,128)(2,1)}, u32[]{:S(2)}, u32[]{:S(2)}) async-start(bf16[16,16,32,128]{3,2,0,1:T(8,128)(2,1)} %copy.43), calls=%async_computation | async-start | bytes 4194304 | tf_op jit(solution)/shard_map/all_to_all | solution.py:90
  155.3 465.1 %all-gather.2.cloned.1.call-start = ((), (), s32[]{:S(2)}) async-start(), calls=%async_computation.5 | async-start | bytes 17825792 | tf_op jit(solution)/shard_map/all_gather | solution.py:124
  161.9 38.3 %copy-start.1 = (bf16[16,16,32,128]{3,2,1,0:T(8,128)(2,1)S(1)}, bf16[16,16,32,128]{3,2,1,0:T(8,128)(2,1)}, u32[]{:S(2)}) copy-start(bf16[16,16,32,128]{3,2,1,0:T(8,128)(2,1)} %copy.46) | copy-start | bytes 6291460
  198.0 2.3 copy-start.2
  208.3 2.6 copy-start
  208.3 9.1 %copy-start.4 = (s32[16,2,10]{0,1,2:T(2,128)S(1)}, s32[16,2,10]{0,1,2:T(2,128)}, u32[]{:S(2)}) copy-start(s32[16,2,10]{0,1,2:T(2,128)} %param.14) | copy-start | bytes 3844
  210.9 214.6 %collective-permute-start = (bf16[2,16,512,128]{3,2,1,0:T(8,128)(2,1)}, bf16[2,16,512,128]{3,2,1,0:T(8,128)(2,1)}, u32[]{:S(2)}, u32[]{:S(2)}) collective-permute-start(bf16[2,16,512,128]{3,2,1,0:T(8,128)(2,1)} %pad_maximum_fusion.1), channel_id=1, source_target_pairs={{0,2},{2,4},{4,6},{6,8},{8,10},{10,12},{12,14},{14,16},{16,18},{18... | collective-permute-start | bytes 12582920 | tf_op jit(solution)/shard_map/ppermute | solution.py:18
  215.7 214.3 %collective-permute-start.1 = (bf16[2,16,512,128]{3,2,1,0:T(8,128)(2,1)}, bf16[2,16,512,128]{3,2,1,0:T(8,128)(2,1)}, u32[]{:S(2)}, u32[]{:S(2)}) collective-permute-start(bf16[2,16,512,128]{3,2,1,0:T(8,128)(2,1)} %pad_maximum_fusion.1), channel_id=1, source_target_pairs={{2,0},{4,2},{6,4},{8,6},{10,8},{12,10},{14,12},{16,14},{18,16},{20... | collective-permute-start | bytes 12582920 | tf_op jit(solution)/shard_map/ppermute | solution.py:20
  217.0 427.5 %reduce-scatter.2.cloned.1.call-start = ((), (), s32[]{:S(2)}) async-start(), calls=%async_computation.6 | async-start | bytes 6291456 | tf_op jit(solution)/shard_map/reduce_scatter | solution.py:127
Sparse Core Ops, SparseCore 0:
  217.2 391.0 all-gather.1
  634.5 9.9 reduce-scatter.1
where the time goes:
time: 653 us; the launch traced here: 651 us
  waiting for transfers between devices  334 us (51%)
  local copies, waits for them, and re-layouts  105 us (16%)
  matrix products  71.2 us (11%)
  blocking collectives  69 us (11%)
  starting transfers between devices  34.9 us (5%)
  other arithmetic  20.7 us (3%)
  between operations  13.6 us (2%)
    ppermute x1, waiting for transfers between devices, extended_2(): lax.ppermute(tail, axis, [(i, (i + 1) % count) for i in range(ends)])  208 us
    all_to_all x1, blocking collectives, shards(): lax.all_to_all(returning, 'seq', split_axis=1, concat_axis=1, tiled=True)  69 us
    all_to_all x1, waiting for transfers between devices, shards(): lax.all_to_all(outgoing(1), 'seq', split_axis=1, concat_axis=1, tiled=True)  39.6 us
    all_to_all x1, waiting for transfers between devices, shards(): lax.all_to_all(outgoing(2), 'seq', split_axis=1, concat_axis=1, tiled=True)  39.1 us
    all_to_all x1, waiting for transfers between devices, shards(): lax.all_to_all(outgoing(0), 'seq', split_axis=1, concat_axis=1, tiled=True)  32.4 us
    dot_general x16, matrix products, attend_head(): jnp.einsum('cqk,ckd->cqd', weights, value_window, preferred_element_type=...  22.5 us
    squeeze x16, local copies, waits for them, and re-layouts, shards(): lax.map(attend_head, (ordered_query, extended[0], extended[1], pattern))  18.8 us
    sub x16, matrix products, attend_head(): exponent = jnp.exp(scores - row_max)  15.5 us
  transfers between devices with their start and end apart: 7, of which 6 were waited for; matrix products, arithmetic and copies ran while one was open for 21% of the time, Pallas kernels for 0%

commit v1 on v0

--- a/solution.py
+++ b/solution.py
@@ -1,6 +1,8 @@
 import jax
 import jax.numpy as jnp
 from jax import lax
+from jax.experimental import pallas as pl
+from jax.experimental.pallas import tpu as pltpu
 from jax.sharding import PartitionSpec as P
 
 CLUSTER = 256
@@ -58,7 +60,7 @@
     return group_of * per_peer + rank
 
 
-def shards(queries, keys, values, route, members, pattern, w_out):
+def slot_shards(queries, keys, values, route, members, pattern, w_out):
     rows_here = queries.shape[0]
     head_count = route.shape[0]
     head_width = queries.shape[1] // head_count
@@ -130,6 +132,280 @@
     return mixed_out
 
 
+LANES = 128
+BLOCK = 128
+
+
+def order_of(key_row):
+    n = key_row.shape[1]
+    key_col = jnp.broadcast_to(key_row, (LANES, n)).T
+    counts = []
+    for j in range(n // LANES):
+        less = key_col < key_row[:, j * LANES : (j + 1) * LANES]
+        counts.append(jnp.sum(jnp.where(less, 1, 0), axis=0, keepdims=True))
+    return jnp.concatenate(counts, axis=1)
+
+
+def table_to(order_row):
+    n = order_row.shape[1]
+    rows = lax.broadcasted_iota(jnp.int32, (n, n), 0)
+    return jnp.where(rows == order_row, 1.0, 0.0).astype(jnp.bfloat16)
+
+
+def table_from(order_row):
+    n = order_row.shape[1]
+    order_col = jnp.broadcast_to(order_row, (LANES, n)).T
+    lane = lax.broadcasted_iota(jnp.int32, (n, LANES), 1)
+    parts = [
+        jnp.where(order_col == lane + j * LANES, 1.0, 0.0).astype(jnp.bfloat16)
+        for j in range(n // LANES)
+    ]
+    return jnp.concatenate(parts, axis=1)
+
+
+def mm(a, b):
+    return jnp.dot(a, b, preferred_element_type=jnp.float32)
+
+
+def pack(route, queries, keys, values):
+    heads, rows = route.shape
+    width = queries.shape[1] // heads
+
+    def kernel(route_ref, q_ref, k_ref, v_ref, out_ref, order_ref):
+        h = pl.program_id(0)
+        order = order_of(route_ref[pl.ds(h, 1), :])
+        order_ref[0] = order
+        table = table_to(order)
+        out_ref[0, 0] = mm(table, q_ref[...]).astype(jnp.bfloat16)
+        out_ref[0, 1] = mm(table, k_ref[...]).astype(jnp.bfloat16)
+        out_ref[0, 2] = mm(table, v_ref[...]).astype(jnp.bfloat16)
+
+    columns = pl.BlockSpec((rows, width), lambda h: (0, h))
+    return pl.pallas_call(
+        kernel,
+        name="pack",
+        grid=(heads,),
+        in_specs=[pl.BlockSpec((heads, rows), lambda h: (0, 0)), columns, columns, columns],
+        out_specs=[
+            pl.BlockSpec((1, 3, rows, width), lambda h: (h, 0, 0, 0)),
+            pl.BlockSpec((1, 1, rows), lambda h: (h, 0, 0)),
+        ],
+        out_shape=[
+            jax.ShapeDtypeStruct((heads, 3, rows, width), jnp.bfloat16),
+            jax.ShapeDtypeStruct((heads, 1, rows), jnp.int32),
+        ],
+    )(route, queries, keys, values)
+
+
+def attend(members, pattern, arrived):
+    nb, rows = members.shape
+    senders, _, _, width = arrived.shape
+    per = rows // senders
+    per_block = rows // CLUSTER
+    window = (2 * REACH + 1) * CLUSTER
+    blocks = window // BLOCK
+    margin = REACH * CLUSTER
+    lag = margin // rows
+    total = nb * rows + 2 * margin
+    scale = width ** (-0.5) * 1.4426950408889634
+
+    def kernel(pat_ref, mem_ref, in_ref, out_ref, kbuf, vbuf, qbuf, arr):
+        g = pl.program_id(0)
+
+        @pl.when(g == 0)
+        def _():
+            zero = jnp.zeros((margin, width), jnp.bfloat16)
+            for at in (0, total - margin):
+                kbuf[at : at + margin, :] = zero
+                vbuf[at : at + margin, :width] = zero
+            vbuf[:, width:] = jnp.ones((total, width), jnp.bfloat16)
+
+        @pl.when(g < nb)
+        def _():
+            row = mem_ref[pl.ds(g, 1), :]
+            slot = lax.broadcasted_iota(jnp.int32, (1, rows), 1)
+            order = order_of(jnp.bitwise_or(jnp.bitwise_and(row, -rows), slot))
+            arr[pl.ds(g % 2, 1)] = order[None]
+            table = table_from(order)
+            at = pl.multiple_of(g * rows + margin, rows)
+            put = [
+                mm(table, in_ref[:, i].reshape(rows, width)).astype(jnp.bfloat16)
+                for i in range(3)
+            ]
+            qbuf[pl.ds(g % 2, 1)] = put[0][None]
+            kbuf[pl.ds(at, rows), :] = put[1]
+            vbuf[pl.ds(at, rows), :width] = put[2]
+
+        @pl.when(g >= lag)
+        def _():
+            b = g - lag
+            contexts = []
+            for i in range(per_block):
+                q = qbuf[pl.ds(b % 2, 1), i * CLUSTER : (i + 1) * CLUSTER, :][0]
+                at = pl.multiple_of(b * rows + i * CLUSTER, CLUSTER)
+                scores = lax.dot_general(
+                    q,
+                    kbuf[pl.ds(at, window), :],
+                    (((1,), (1,)), ((), ())),
+                    preferred_element_type=jnp.float32,
+                )
+                parts = []
+                for j in range(blocks):
+                    allowed = pat_ref[(b * per_block + i) * blocks + j] > 0
+                    shift = jnp.where(allowed, 0.0, -jnp.inf)
+                    parts.append(scores[:, j * BLOCK : (j + 1) * BLOCK] + shift)
+                most = parts[0]
+                for part in parts[1:]:
+                    most = jnp.maximum(most, part)
+                most = jnp.max(most, axis=1, keepdims=True)
+                weights = jnp.concatenate(
+                    [jnp.exp2((part - most) * scale).astype(jnp.bfloat16) for part in parts], axis=1
+                )
+                both = mm(weights, vbuf[pl.ds(at, window), :])
+                contexts.append((both[:, :width] / both[:, width:]).astype(jnp.bfloat16))
+            context = jnp.concatenate(contexts, axis=0)
+            back = mm(table_to(arr[pl.ds(b % 2, 1)][0]), context).astype(jnp.bfloat16)
+            out_ref[...] = back.reshape(senders, per, width)
+
+    return pl.pallas_call(
+        kernel,
+        name="attend",
+        grid_spec=pltpu.PrefetchScalarGridSpec(
+            num_scalar_prefetch=1,
+            grid=(nb + lag,),
+            in_specs=[
+                pl.BlockSpec((nb, rows), lambda g, p: (0, 0)),
+                pl.BlockSpec((senders, 3, per, width), lambda g, p: (0, 0, jnp.minimum(g, nb - 1), 0)),
+            ],
+            out_specs=pl.BlockSpec((senders, per, width), lambda g, p: (0, jnp.maximum(g - lag, 0), 0)),
+            scratch_shapes=[
+                pltpu.VMEM((total, width), jnp.bfloat16),
+                pltpu.VMEM((total, 2 * width), jnp.bfloat16),
+                pltpu.VMEM((2, rows, width), jnp.bfloat16),
+                pltpu.VMEM((2, 1, rows), jnp.int32),
+            ],
+        ),
+        out_shape=jax.ShapeDtypeStruct((senders, nb * per, width), jnp.bfloat16),
+    )(pattern, members, arrived)
+
+
+def unpack(order, returned):
+    heads, rows, width = returned.shape
+
+    def kernel(order_ref, in_ref, out_ref):
+        out_ref[...] = mm(table_from(order_ref[0]), in_ref[0]).astype(jnp.bfloat16)
+
+    return pl.pallas_call(
+        kernel,
+        name="unpack",
+        grid=(heads,),
+        in_specs=[
+            pl.BlockSpec((1, 1, rows), lambda h: (h, 0, 0)),
+            pl.BlockSpec((1, rows, width), lambda h: (h, 0, 0)),
+        ],
+        out_specs=pl.BlockSpec((rows, width), lambda h: (0, h)),
+        out_shape=jax.ShapeDtypeStruct((rows, heads * width), jnp.bfloat16),
+    )(order, returned)
+
+
+def project(pieces, pieces_too, attended, first, second):
+    count = pieces.shape[0]
+    rows, depth = attended.shape
+    half, cols = first.shape[1:]
+
+    def kernel(at_ref, too_ref, a_ref, f_ref, s_ref, out_ref):
+        out_ref[...] = (mm(a_ref[:, :half], f_ref[0]) + mm(a_ref[:, half:], s_ref[0])).astype(
+            jnp.bfloat16
+        )
+
+    return pl.pallas_call(
+        kernel,
+        name="project",
+        grid_spec=pltpu.PrefetchScalarGridSpec(
+            num_scalar_prefetch=2,
+            grid=(count,),
+            in_specs=[
+                pl.BlockSpec((rows, depth), lambda j, at, too: (0, 0)),
+                pl.BlockSpec((1, half, cols), lambda j, at, too: (at[j], 0, 0)),
+                pl.BlockSpec((1, half, cols), lambda j, at, too: (too[j], 0, 0)),
+            ],
+            out_specs=pl.BlockSpec((rows, cols), lambda j, at, too: (0, j)),
+        ),
+        out_shape=jax.ShapeDtypeStruct((rows, count * cols), jnp.bfloat16),
+    )(pieces, pieces_too, attended, first, second)
+
+
+def gather_weights(w_out):
+    count = lax.axis_size("seq")
+    line = count // 4
+    me = lax.axis_index("seq")
+    right = [(i, i + 4) for i in range(count - 4)]
+    left = [(i + 4, i) for i in range(count - 4)]
+    from_left, from_right = [w_out], [w_out]
+    for _ in range(line - 1):
+        from_left.append(lax.ppermute(from_left[-1], "seq", right))
+        from_right.append(lax.ppermute(from_right[-1], "seq", left))
+    stack = [w_out] + [from_left[k] + from_right[line - k] for k in range(1, line)]
+    half = w_out.shape[0] // 2
+
+    def doubled(cells, bit):
+        other = lax.ppermute(cells, "seq", [(i, i ^ bit) for i in range(count)])
+        return jnp.concatenate([cells, other], axis=0)
+
+    first = doubled(doubled(jnp.stack([cell[:half] for cell in stack]), 2), 1)
+    second = doubled(doubled(jnp.stack([cell[half:] for cell in stack]), 1), 2)
+    names = jnp.arange(count, dtype=jnp.int32)
+    step = jnp.mod(me // 4 - names // 4, line)
+    differ = jnp.bitwise_xor(me, names)
+    low, high = differ % 2, (differ // 2) % 2
+    return first, second, (low * 2 + high) * line + step, (high * 2 + low) * line + step
+
+
+def head_shards(queries, keys, values, route, members, pattern, w_out):
+    heads, rows = route.shape
+    count = lax.axis_size("seq")
+    extra = pattern.shape[1] * pattern.shape[2]
+    meta = jnp.concatenate(
+        [
+            members,
+            pattern.reshape(heads, extra),
+            jnp.zeros((heads, LANES - extra), jnp.int32),
+        ],
+        axis=1,
+    )
+    meta = lax.all_to_all(meta, "seq", split_axis=0, concat_axis=0, tiled=True)
+    packed, order = pack(route, queries, keys, values)
+    arrived = lax.all_to_all(packed, "seq", split_axis=0, concat_axis=0, tiled=True)
+    first, second, at_first, at_second = gather_weights(w_out)
+    context = attend(meta[:, :rows], meta[:, rows : rows + extra].reshape(-1), arrived)
+    returned = lax.all_to_all(context, "seq", split_axis=0, concat_axis=0, tiled=True)
+    attended = unpack(order, returned)
+    mine = lax.axis_index("tp")
+    half = count // 2
+
+    def part(which):
+        places = [lax.dynamic_slice_in_dim(at, which * half, half) for at in (at_first, at_second)]
+        return project(places[0], places[1], attended, first, second)
+
+    send = part(1 - mine)
+    received = lax.ppermute(send, "tp", [(0, 1), (1, 0)])
+    keep = part(mine)
+    return (keep.astype(jnp.float32) + received.astype(jnp.float32)).astype(jnp.bfloat16)
+
+
+def choose(mesh):
+    count, groups = mesh.shape["seq"], mesh.shape["tp"]
+
+    def shards(queries, keys, values, route, members, pattern, w_out):
+        heads, rows = route.shape
+        split = heads == count and groups == 2 and count % 4 == 0
+        tiles = rows == REACH * CLUSTER and queries.shape[1] == heads * LANES
+        body = head_shards if split and tiles else slot_shards
+        return body(queries, keys, values, route, members, pattern, w_out)
+
+    return shards
+
+
 def solution(mesh):
     placed = (
         P("seq", "tp"),
@@ -141,5 +417,5 @@
         P("tp", "seq"),
     )
     return jax.shard_map(
-        shards, mesh=mesh, in_specs=placed, out_specs=P("seq", "tp"), check_vma=False
-    )
+        choose(mesh), mesh=mesh, in_specs=placed, out_specs=P("seq", "tp"), check_vma=False
+    )

time: 653 us -> 457 us (0.70)
  Pallas kernels: 0 us -> 90.7 us
  waiting for transfers between devices: 334 us -> 252 us
  local copies, waits for them, and re-layouts: 105 us -> 24.9 us
  matrix products: 71.2 us -> 0 us
  blocking collectives: 69 us -> 0 us
  starting transfers between devices: 34.9 us -> 81.1 us
  other arithmetic: 20.7 us -> 5.93 us
  between operations: 13.6 us -> 0.2 us
    all_to_all x3, waiting for transfers between devices: 111 us -> 0.01 us  [the longest x1 0.01 us: head_shards(): lax.all_to_all(packed, 'seq', split_axis=0, concat_axis=0, tiled=True)]
    pallas_call x0 -> x5, Pallas kernels: none -> 90.7 us  [the longest x1 39.8 us: attend(): pl.pallas_call(kernel, name='attend', grid_spec=pltpu.PrefetchScalarGridS...]
    all_to_all x1 -> x0, blocking collectives: 69 us -> none  [shards(): lax.all_to_all(returning, 'seq', split_axis=1, concat_axis=1, tiled=True)]
    dot_general x21 -> x0, matrix products: 55.7 us -> none  [the longest x16 22.5 us: attend_head(): jnp.einsum('cqk,ckd->cqd', weights, value_window, preferred_element_type=...]
    ppermute x2 -> x11, starting transfers between devices: 6.15 us -> 60 us  [the longest x3 47.1 us: gather_weights(): from_left.append(lax.ppermute(from_left[-1], 'seq', right))]
    ppermute x2 -> x11, waiting for transfers between devices: 213 us -> 252 us  [the longest x3 159 us: gather_weights(): from_right.append(lax.ppermute(from_right[-1], 'seq', left))]
    squeeze x17 -> x0, local copies, waits for them, and re-layouts: 24.3 us -> none  [the longest x16 18.8 us: shards(): lax.map(attend_head, (ordered_query, extended[0], extended[1], pattern))]
    reshape x7 -> x2, local copies, waits for them, and re-layouts: 16.5 us -> 0.76 us  [the longest x1 0.68 us: head_shards(): meta[:, rows:rows + extra].reshape(-1)]
  transfers between devices with their start and end apart: 7 -> 14, of which waited for: 6 -> 6; matrix products, arithmetic and copies ran while one was open for 21% -> 5% of each run, Pallas kernels for 0% -> 15%
where the time goes in v1:
time: 457 us; the launch traced here: 455 us
  waiting for transfers between devices  252 us (55%)
  Pallas kernels  90.7 us (20%)
  starting transfers between devices  81.1 us (18%)
  local copies, waits for them, and re-layouts  24.9 us (5%)
  other arithmetic  5.93 us (1%)
    ppermute x3, waiting for transfers between devices, gather_weights(): from_right.append(lax.ppermute(from_right[-1], 'seq', left))  159 us
    ppermute x4, waiting for transfers between devices, doubled(): other = lax.ppermute(cells, 'seq', [(i, i ^ bit) for i in range(count)])  92.3 us
    ppermute x3, starting transfers between devices, gather_weights(): from_left.append(lax.ppermute(from_left[-1], 'seq', right))  47.1 us
    pallas_call x1, Pallas kernels, attend(): pl.pallas_call(kernel, name='attend', grid_spec=pltpu.PrefetchScalarGridS...  39.8 us
    pallas_call x2, Pallas kernels, project(): pl.pallas_call(kernel, name='project', grid_spec=pltpu.PrefetchScalarGrid...  22.2 us
    pallas_call x1, Pallas kernels, pack(): pl.pallas_call(kernel, name='pack', grid=(heads,), in_specs=[pl.BlockSpec...  16.8 us
    concatenate x4, local copies, waits for them, and re-layouts, doubled(): return jnp.concatenate([cells, other], axis=0)  13.4 us
    pallas_call x1, Pallas kernels, unpack(): pl.pallas_call(kernel, name='unpack', grid=(heads,), in_specs=[pl.BlockSp...  11.8 us
  transfers between devices with their start and end apart: 14, of which 6 were waited for; matrix products, arithmetic and copies ran while one was open for 5% of the time, Pallas kernels for 15%

profile of v1, /device:TPU:0, one launch (start us, length us, event | category | flops | bytes accessed | tf_op | source)
XLA Modules:
  0.0 454.9 jit_solution(13671013589896080039)
XLA Ops:
  2.4 8.3 %all-to-all-start = ((s32[16,1,640]{2,1,0:T(1,128)}), s32[16,1,640]{2,1,0:T(1,128)S(1)}, u32[]{:S(2)}, u32[]{:S(2)}) async-start(s32[16,1,640]{2,1,0:T(1,128)} %all_to_all.14), calls=%async_computation | async-start | bytes 81920 | tf_op jit(solution)/shard_map/all_to_all | solution.py:376
  10.7 16.8 %pack.1 = (bf16[16,3,512,128]{3,2,1,0:T(8,128)(2,1)}, s32[16,1,512]{2,1,0:T(1,128)}) custom-call(s32[16,512]{1,0:T(8,128)} %route_ref.1, bf16[512,2048]{1,0:T(8,128)(2,1)} %q_ref.1, bf16[512,2048]{1,0:T(8,128)(2,1)} %k_ref.1, bf16[512,2048]{1,0:T(8,128)(2,1)} %v_ref.1), custom_call_target="tpu_custom_call" | custom-call | tf_op jit(solution)/shard_map/pack/pallas_call | solution.py:184
  27.6 7.1 %all-to-all-start.1 = ((bf16[16,3,512,128]{3,2,1,0:T(8,128)(2,1)}), bf16[16,3,512,128]{3,2,1,0:T(8,128)(2,1)}, u32[]{:S(2)}, u32[]{:S(2)}) async-start(bf16[16,3,512,128]{3,2,1,0:T(8,128)(2,1)} %get-tuple-element.8), calls=%async_computation.1 | async-start | bytes 12582912 | tf_op jit(solution)/shard_map/all_to_all | solution.py:378
  34.7 1.3 collective-permute-start.1
  36.0 4.6 %collective-permute-start = (bf16[2048,256]{1,0:T(8,128)(2,1)S(1)}, bf16[2048,256]{1,0:T(8,128)(2,1)S(1)}, u32[]{:S(2)}, u32[]{:S(2)}) collective-permute-start(bf16[2048,256]{1,0:T(8,128)(2,1)S(1)} %copy-done.1), channel_id=1, source_target_pairs={{0,8},{2,10},{4,12},{6,14},{8,16},{10,18},{12,20},{14,22},{16,24},... | collective-permute-start | bytes 3145736 | tf_op jit(solution)/shard_map/ppermute | solution.py:346
  40.6 119.3 %collective-permute-done.1 = bf16[2048,256]{1,0:T(8,128)(2,1)S(1)} collective-permute-done((bf16[2048,256]{1,0:T(8,128)(2,1)S(1)}, bf16[2048,256]{1,0:T(8,128)(2,1)S(1)}, u32[]{:S(2)}, u32[]{:S(2)}) %collective-permute-start.1) | collective-permute-done | bytes 1048608 | tf_op jit(solution)/shard_map/ppermute | solution.py:347
  159.9 1.3 collective-permute-start.2
  161.2 37.9 %collective-permute-start.4 = (bf16[2048,256]{1,0:T(8,128)(2,1)S(1)}, bf16[2048,256]{1,0:T(8,128)(2,1)S(1)}, u32[]{:S(2)}, u32[]{:S(2)}) collective-permute-start(bf16[2048,256]{1,0:T(8,128)(2,1)S(1)} %collective-permute-done), channel_id=1, source_target_pairs={{0,8},{2,10},{4,12},{6,14},{8,16},{10,18},{12,20},{14,22},{16,24},... | collective-permute-start | bytes 3145736 | tf_op jit(solution)/shard_map/ppermute | solution.py:346
  199.1 20.4 %collective-permute-done.2 = bf16[2048,256]{1,0:T(8,128)(2,1)S(1)} collective-permute-done((bf16[2048,256]{1,0:T(8,128)(2,1)S(1)}, bf16[2048,256]{1,0:T(8,128)(2,1)S(1)}, u32[]{:S(2)}, u32[]{:S(2)}) %collective-permute-start.2) | collective-permute-done | bytes 1048608 | tf_op jit(solution)/shard_map/ppermute | solution.py:347
  219.5 1.3 collective-permute-start.3
  220.8 4.6 %collective-permute-start.5 = (bf16[2048,256]{1,0:T(8,128)(2,1)S(1)}, bf16[2048,256]{1,0:T(8,128)(2,1)S(1)}, u32[]{:S(2)}, u32[]{:S(2)}) collective-permute-start(bf16[2048,256]{1,0:T(8,128)(2,1)S(1)} %collective-permute-done.4), channel_id=1, source_target_pairs={{0,8},{2,10},{4,12},{6,14},{8,16},{10,18},{12,20},{14,22},{16,24},... | collective-permute-start | bytes 3145736 | tf_op jit(solution)/shard_map/ppermute | solution.py:346
  225.9 19.1 %collective-permute-done.3 = bf16[2048,256]{1,0:T(8,128)(2,1)S(1)} collective-permute-done((bf16[2048,256]{1,0:T(8,128)(2,1)S(1)}, bf16[2048,256]{1,0:T(8,128)(2,1)S(1)}, u32[]{:S(2)}, u32[]{:S(2)}) %collective-permute-start.3) | collective-permute-done | bytes 1048608 | tf_op jit(solution)/shard_map/ppermute | solution.py:347
  246.9 4.2 collective-permute-start.8
  251.4 1.5 collective-permute-start.6
  252.9 1.5 constant_dynamic-update-slice_fusion.15
  254.3 1.4 constant_dynamic-update-slice_fusion.14
  255.7 1.4 constant_dynamic-update-slice_fusion.13
  257.2 1.4 constant_dynamic-update-slice_fusion.12
  258.6 35.7 %collective-permute-done.8 = bf16[4,1024,256]{2,1,0:T(8,128)(2,1)S(1)} collective-permute-done((bf16[4,1024,256]{2,1,0:T(8,128)(2,1)S(1)}, bf16[4,1024,256]{2,1,0:T(8,128)(2,1)S(1)}, u32[]{:S(2)}, u32[]{:S(2)}) %collective-permute-start.8) | collective-permute-done | bytes 2097184 | tf_op jit(solution)/shard_map/ppermute | solution.py:352
  294.3 2.3 constant_dynamic-update-slice_fusion.11
  296.6 3.1 collective-permute-start.9
  299.7 2.3 constant_dynamic-update-slice_fusion
  303.6 39.8 %attend.1 = bf16[16,512,128]{2,1,0:T(8,128)(2,1)} custom-call(s32[320]{0:T(512)} %reshape.9.pat_ref, s32[16,512]{1,0:T(8,128)} %slice.41.mem_ref, bf16[16,3,512,128]{3,2,1,0:T(8,128)(2,1)} %all-to-all-done.1.in_ref), custom_call_target="tpu_custom_call" | custom-call | tf_op jit(solution)/shard_map/attend/pallas_call | solution.py:270
  343.4 5.7 %all-to-all-start.2 = ((bf16[16,512,128]{2,1,0:T(8,128)(2,1)}), bf16[16,512,128]{2,1,0:T(8,128)(2,1)S(1)}, u32[]{:S(2)}, u32[]{:S(2)}) async-start(bf16[16,512,128]{2,1,0:T(8,128)(2,1)} %attend.1), calls=%async_computation.2 | async-start | bytes 4194304 | tf_op jit(solution)/shard_map/all_to_all | solution.py:381
  350.3 56.6 %collective-permute-done.9 = bf16[8,1024,256]{2,1,0:T(8,128)(2,1)} collective-permute-done((bf16[8,1024,256]{2,1,0:T(8,128)(2,1)}, bf16[8,1024,256]{2,1,0:T(8,128)(2,1)}, u32[]{:S(2)}, u32[]{:S(2)}) %collective-permute-start.9) | collective-permute-done | bytes 4194336 | tf_op jit(solution)/shard_map/ppermute | solution.py:352
  406.9 4.5 constant_dynamic-update-slice_fusion.16.s_ref
  411.4 4.4 constant_dynamic-update-slice_fusion.5.f_ref
  415.8 1.3 copy-done
  417.1 11.8 %unpack.1.a_ref = bf16[512,2048]{1,0:T(8,128)(2,1)} custom-call(s32[16,1,512]{2,1,0:T(1,128)} %get-tuple-element.7.order_ref, bf16[16,512,128]{2,1,0:T(8,128)(2,1)} %copy-done), custom_call_target="tpu_custom_call" | custom-call | tf_op jit(solution)/shard_map/unpack/pallas_call | solution.py:298
  429.0 11.1 %project.3 = bf16[512,2048]{1,0:T(8,128)(2,1)} custom-call(s32[8]{0:T(128)} %get-tuple-element.40.at_ref, s32[8]{0:T(128)} %get-tuple-element.38.too_ref, bf16[512,2048]{1,0:T(8,128)(2,1)} %unpack.1.a_ref, bf16[16,1024,256]{2,1,0:T(8,128)(2,1)} %constant_dynamic-update-slice_fusion.5.f_ref, bf16[16,1024,256]{2,1,0:T(8,128)(2,1)} %constant_dynamic-update-slice_fusion.16.s_ref), custom_call_target="tpu_custom_call" | custom-call | tf_op jit(solution)/shard_map/project/pallas_call | solution.py:321
  440.1 11.1 %project.2 = bf16[512,2048]{1,0:T(8,128)(2,1)} custom-call(s32[8]{0:T(128)} %get-tuple-element.39.at_ref, s32[8]{0:T(128)} %get-tuple-element.37.too_ref, bf16[512,2048]{1,0:T(8,128)(2,1)} %unpack.1.a_ref, bf16[16,1024,256]{2,1,0:T(8,128)(2,1)} %constant_dynamic-update-slice_fusion.5.f_ref, bf16[16,1024,256]{2,1,0:T(8,128)(2,1)} %constant_dynamic-update-slice_fusion.16.s_ref), custom_call_target="tpu_custom_call" | custom-call | tf_op jit(solution)/shard_map/project/pallas_call | solution.py:321
  451.2 3.7 add_convert_fusion
  (36 shorter events, 7.9 us)
Async XLA Ops:
  2.4 25.2 %all-to-all-start = ((s32[16,1,640]{2,1,0:T(1,128)}), s32[16,1,640]{2,1,0:T(1,128)S(1)}, u32[]{:S(2)}, u32[]{:S(2)}) async-start(s32[16,1,640]{2,1,0:T(1,128)} %all_to_all.14), calls=%async_computation | async-start | bytes 81920 | tf_op jit(solution)/shard_map/all_to_all | solution.py:376
  27.5 7.1 %copy-start.1 = (bf16[2048,256]{1,0:T(8,128)(2,1)S(1)}, bf16[2048,256]{1,0:T(8,128)(2,1)}, u32[]{:S(2)}) copy-start(bf16[2048,256]{1,0:T(8,128)(2,1)} %param.13) | copy-start | bytes 3145732
  27.6 276.0 %all-to-all-start.1 = ((bf16[16,3,512,128]{3,2,1,0:T(8,128)(2,1)}), bf16[16,3,512,128]{3,2,1,0:T(8,128)(2,1)}, u32[]{:S(2)}, u32[]{:S(2)}) async-start(bf16[16,3,512,128]{3,2,1,0:T(8,128)(2,1)} %get-tuple-element.8), calls=%async_computation.1 | async-start | bytes 12582912 | tf_op jit(solution)/shard_map/all_to_all | solution.py:378
  34.7 125.2 %collective-permute-start.1 = (bf16[2048,256]{1,0:T(8,128)(2,1)S(1)}, bf16[2048,256]{1,0:T(8,128)(2,1)S(1)}, u32[]{:S(2)}, u32[]{:S(2)}) collective-permute-start(bf16[2048,256]{1,0:T(8,128)(2,1)S(1)} %copy-done.1), channel_id=1, source_target_pairs={{8,0},{10,2},{12,4},{14,6},{16,8},{18,10},{20,12},{22,14},{24,16},... | collective-permute-start | bytes 3145736 | tf_op jit(solution)/shard_map/ppermute | solution.py:347
  36.0 125.2 %collective-permute-start = (bf16[2048,256]{1,0:T(8,128)(2,1)S(1)}, bf16[2048,256]{1,0:T(8,128)(2,1)S(1)}, u32[]{:S(2)}, u32[]{:S(2)}) collective-permute-start(bf16[2048,256]{1,0:T(8,128)(2,1)S(1)} %copy-done.1), channel_id=1, source_target_pairs={{0,8},{2,10},{4,12},{6,14},{8,16},{10,18},{12,20},{14,22},{16,24},... | collective-permute-start | bytes 3145736 | tf_op jit(solution)/shard_map/ppermute | solution.py:346
  159.9 59.6 %collective-permute-start.2 = (bf16[2048,256]{1,0:T(8,128)(2,1)S(1)}, bf16[2048,256]{1,0:T(8,128)(2,1)S(1)}, u32[]{:S(2)}, u32[]{:S(2)}) collective-permute-start(bf16[2048,256]{1,0:T(8,128)(2,1)S(1)} %collective-permute-done.1), channel_id=1, source_target_pairs={{8,0},{10,2},{12,4},{14,6},{16,8},{18,10},{20,12},{22,14},{24,16},... | collective-permute-start | bytes 3145736 | tf_op jit(solution)/shard_map/ppermute | solution.py:347
  161.2 59.6 %collective-permute-start.4 = (bf16[2048,256]{1,0:T(8,128)(2,1)S(1)}, bf16[2048,256]{1,0:T(8,128)(2,1)S(1)}, u32[]{:S(2)}, u32[]{:S(2)}) collective-permute-start(bf16[2048,256]{1,0:T(8,128)(2,1)S(1)} %collective-permute-done), channel_id=1, source_target_pairs={{0,8},{2,10},{4,12},{6,14},{8,16},{10,18},{12,20},{14,22},{16,24},... | collective-permute-start | bytes 3145736 | tf_op jit(solution)/shard_map/ppermute | solution.py:346
  219.5 25.5 %collective-permute-start.3 = (bf16[2048,256]{1,0:T(8,128)(2,1)S(1)}, bf16[2048,256]{1,0:T(8,128)(2,1)S(1)}, u32[]{:S(2)}, u32[]{:S(2)}) collective-permute-start(bf16[2048,256]{1,0:T(8,128)(2,1)S(1)} %collective-permute-done.2), channel_id=1, source_target_pairs={{8,0},{10,2},{12,4},{14,6},{16,8},{18,10},{20,12},{22,14},{24,16},... | collective-permute-start | bytes 3145736 | tf_op jit(solution)/shard_map/ppermute | solution.py:347
  220.8 25.4 %collective-permute-start.5 = (bf16[2048,256]{1,0:T(8,128)(2,1)S(1)}, bf16[2048,256]{1,0:T(8,128)(2,1)S(1)}, u32[]{:S(2)}, u32[]{:S(2)}) collective-permute-start(bf16[2048,256]{1,0:T(8,128)(2,1)S(1)} %collective-permute-done.4), channel_id=1, source_target_pairs={{0,8},{2,10},{4,12},{6,14},{8,16},{10,18},{12,20},{14,22},{16,24},... | collective-permute-start | bytes 3145736 | tf_op jit(solution)/shard_map/ppermute | solution.py:346
  246.9 47.4 %collective-permute-start.8 = (bf16[4,1024,256]{2,1,0:T(8,128)(2,1)S(1)}, bf16[4,1024,256]{2,1,0:T(8,128)(2,1)S(1)}, u32[]{:S(2)}, u32[]{:S(2)}) collective-permute-start(bf16[4,1024,256]{2,1,0:T(8,128)(2,1)S(1)} %pad_maximum_fusion.1), channel_id=1, source_target_pairs={{0,2},{2,0},{4,6},{6,4},{8,10},{10,8},{12,14},{14,12},{16,18},{18,... | collective-permute-start | bytes 6291464 | tf_op jit(solution)/shard_map/ppermute | solution.py:352
  251.4 48.3 %collective-permute-start.6 = (bf16[4,1024,256]{2,1,0:T(8,128)(2,1)S(1)}, bf16[4,1024,256]{2,1,0:T(8,128)(2,1)S(1)}, u32[]{:S(2)}, u32[]{:S(2)}) collective-permute-start(bf16[4,1024,256]{2,1,0:T(8,128)(2,1)S(1)} %pad_maximum_fusion), channel_id=1, source_target_pairs={{0,4},{2,6},{4,0},{6,2},{8,12},{10,14},{12,8},{14,10},{16,20},{18,... | collective-permute-start | bytes 6291464 | tf_op jit(solution)/shard_map/ppermute | solution.py:352
  296.6 110.4 %collective-permute-start.9 = (bf16[8,1024,256]{2,1,0:T(8,128)(2,1)}, bf16[8,1024,256]{2,1,0:T(8,128)(2,1)}, u32[]{:S(2)}, u32[]{:S(2)}) collective-permute-start(bf16[8,1024,256]{2,1,0:T(8,128)(2,1)} %get-tuple-element.9), channel_id=1, source_target_pairs={{0,4},{2,6},{4,0},{6,2},{8,12},{10,14},{12,8},{14,10},{16,20},{18,... | collective-permute-start | bytes 12582920 | tf_op jit(solution)/shard_map/ppermute | solution.py:352
  302.0 109.4 %collective-permute-start.7 = (bf16[8,1024,256]{2,1,0:T(8,128)(2,1)}, bf16[8,1024,256]{2,1,0:T(8,128)(2,1)}, u32[]{:S(2)}, u32[]{:S(2)}) collective-permute-start(bf16[8,1024,256]{2,1,0:T(8,128)(2,1)} %get-tuple-element.11), channel_id=1, source_target_pairs={{0,2},{2,0},{4,6},{6,4},{8,10},{10,8},{12,14},{14,12},{16,18},{18,... | collective-permute-start | bytes 12582920 | tf_op jit(solution)/shard_map/ppermute | solution.py:352
  343.4 72.4 %all-to-all-start.2 = ((bf16[16,512,128]{2,1,0:T(8,128)(2,1)}), bf16[16,512,128]{2,1,0:T(8,128)(2,1)S(1)}, u32[]{:S(2)}, u32[]{:S(2)}) async-start(bf16[16,512,128]{2,1,0:T(8,128)(2,1)} %attend.1), calls=%async_computation.2 | async-start | bytes 4194304 | tf_op jit(solution)/shard_map/all_to_all | solution.py:381
  415.8 1.3 copy-start
  440.1 11.1 %collective-permute-start.10 = (bf16[512,2048]{1,0:T(8,128)(2,1)}, bf16[512,2048]{1,0:T(8,128)(2,1)S(1)}, u32[]{:S(2)}, u32[]{:S(2)}) collective-permute-start(bf16[512,2048]{1,0:T(8,128)(2,1)} %project.3), channel_id=1, source_target_pairs={{0,1},{1,0},{2,3},{3,2},{4,5},{5,4},{6,7},{7,6},{8,9},{9,8},{10,11... | collective-permute-start | bytes 6291464 | tf_op jit(solution)/shard_map/ppermute | solution.py:391

commit v2 on v1

--- a/solution.py
+++ b/solution.py
@@ -4,6 +4,7 @@
 from jax.experimental import pallas as pl
 from jax.experimental.pallas import tpu as pltpu
 from jax.sharding import PartitionSpec as P
+
 
 CLUSTER = 256
 REACH = 2
@@ -133,6 +134,8 @@
 
 
 LANES = 128
+DIGIT = 4
+TAIL = 32
 BLOCK = 128
 
 
@@ -167,39 +170,72 @@
     return jnp.dot(a, b, preferred_element_type=jnp.float32)
 
 
-def pack(route, queries, keys, values):
+def pack(route, pattern, queries, keys, values):
     heads, rows = route.shape
     width = queries.shape[1] // heads
-
-    def kernel(route_ref, q_ref, k_ref, v_ref, out_ref, order_ref):
+    lines = rows // LANES
+
+    def kernel(route_ref, pat_ref, q_ref, k_ref, v_ref, out_ref, order_ref):
         h = pl.program_id(0)
-        order = order_of(route_ref[pl.ds(h, 1), :])
+        row = route_ref[pl.ds(h, 1), :]
+        order = order_of(row)
         order_ref[0] = order
         table = table_to(order)
-        out_ref[0, 0] = mm(table, q_ref[...]).astype(jnp.bfloat16)
-        out_ref[0, 1] = mm(table, k_ref[...]).astype(jnp.bfloat16)
-        out_ref[0, 2] = mm(table, v_ref[...]).astype(jnp.bfloat16)
+        out_ref[0, 0:rows] = mm(table, q_ref[...]).astype(jnp.bfloat16)
+        out_ref[0, rows : 2 * rows] = mm(table, k_ref[...]).astype(jnp.bfloat16)
+        out_ref[0, 2 * rows : 3 * rows] = mm(table, v_ref[...]).astype(jnp.bfloat16)
+        slot = jnp.bitwise_and(row, rows - 1)
+        high = lax.shift_right_logical(slot, DIGIT)
+        low = jnp.bitwise_and(slot, (1 << DIGIT) - 1)
+        at = lax.broadcasted_iota(jnp.int32, (8, rows), 0)
+        digits = jnp.where(at == 0, high, jnp.where(at == 1, low, 0))
+        digits = digits.astype(jnp.float32).astype(jnp.bfloat16)
+        sorted_digits = lax.dot_general(
+            digits, table, (((1,), (1,)), ((), ())), preferred_element_type=jnp.float32
+        )
+        parts = [
+            sorted_digits[d : d + 1, j * LANES : (j + 1) * LANES] for d in range(2) for j in range(lines)
+        ]
+        parts.append(pat_ref[pl.ds(h, 1), :].astype(jnp.float32))
+        parts.append(jnp.zeros((TAIL - 2 * lines - 1, LANES), jnp.float32))
+        out_ref[0, 3 * rows :] = jnp.concatenate(parts, axis=0).astype(jnp.bfloat16)
 
     columns = pl.BlockSpec((rows, width), lambda h: (0, h))
+    total = 3 * rows + TAIL
     return pl.pallas_call(
         kernel,
         name="pack",
         grid=(heads,),
-        in_specs=[pl.BlockSpec((heads, rows), lambda h: (0, 0)), columns, columns, columns],
+        in_specs=[
+            pl.BlockSpec((heads, rows), lambda h: (0, 0)),
+            pl.BlockSpec((heads, LANES), lambda h: (0, 0)),
+            columns,
+            columns,
+            columns,
+        ],
         out_specs=[
-            pl.BlockSpec((1, 3, rows, width), lambda h: (h, 0, 0, 0)),
+            pl.BlockSpec((1, total, width), lambda h: (h, 0, 0)),
             pl.BlockSpec((1, 1, rows), lambda h: (h, 0, 0)),
         ],
         out_shape=[
-            jax.ShapeDtypeStruct((heads, 3, rows, width), jnp.bfloat16),
+            jax.ShapeDtypeStruct((heads, total, width), jnp.bfloat16),
             jax.ShapeDtypeStruct((heads, 1, rows), jnp.int32),
         ],
-    )(route, queries, keys, values)
-
-
-def attend(members, pattern, arrived):
-    nb, rows = members.shape
-    senders, _, _, width = arrived.shape
+    )(route, pattern, queries, keys, values)
+
+
+def tail_of(arrived, rows, entries):
+    senders = arrived.shape[0]
+    lines = rows // LANES
+    tail = arrived[:, 3 * rows : 3 * rows + 2 * lines + 1].astype(jnp.int32)
+    slot = (tail[:, :lines] << DIGIT) + tail[:, lines : 2 * lines]
+    slot = slot.reshape(senders, senders, rows // senders).transpose(1, 0, 2)
+    return slot.reshape(senders, rows), tail[:, 2 * lines, :entries].reshape(-1)
+
+
+def attend(slots, pattern, arrived):
+    nb, rows = slots.shape
+    senders, _, width = arrived.shape
     per = rows // senders
     per_block = rows // CLUSTER
     window = (2 * REACH + 1) * CLUSTER
@@ -209,7 +245,7 @@
     total = nb * rows + 2 * margin
     scale = width ** (-0.5) * 1.4426950408889634
 
-    def kernel(pat_ref, mem_ref, in_ref, out_ref, kbuf, vbuf, qbuf, arr):
+    def kernel(pat_ref, slot_ref, q_ref, k_ref, v_ref, out_ref, kbuf, vbuf, qbuf):
         g = pl.program_id(0)
 
         @pl.when(g == 0)
@@ -222,15 +258,11 @@
 
         @pl.when(g < nb)
         def _():
-            row = mem_ref[pl.ds(g, 1), :]
-            slot = lax.broadcasted_iota(jnp.int32, (1, rows), 1)
-            order = order_of(jnp.bitwise_or(jnp.bitwise_and(row, -rows), slot))
-            arr[pl.ds(g % 2, 1)] = order[None]
-            table = table_from(order)
+            table = table_to(slot_ref[pl.ds(g, 1), :])
             at = pl.multiple_of(g * rows + margin, rows)
             put = [
-                mm(table, in_ref[:, i].reshape(rows, width)).astype(jnp.bfloat16)
-                for i in range(3)
+                mm(table, ref[...].reshape(rows, width)).astype(jnp.bfloat16)
+                for ref in (q_ref, k_ref, v_ref)
             ]
             qbuf[pl.ds(g % 2, 1)] = put[0][None]
             kbuf[pl.ds(at, rows), :] = put[1]
@@ -264,7 +296,7 @@
                 both = mm(weights, vbuf[pl.ds(at, window), :])
                 contexts.append((both[:, :width] / both[:, width:]).astype(jnp.bfloat16))
             context = jnp.concatenate(contexts, axis=0)
-            back = mm(table_to(arr[pl.ds(b % 2, 1)][0]), context).astype(jnp.bfloat16)
+            back = mm(table_from(slot_ref[pl.ds(b, 1), :]), context).astype(jnp.bfloat16)
             out_ref[...] = back.reshape(senders, per, width)
 
     return pl.pallas_call(
@@ -275,18 +307,23 @@
             grid=(nb + lag,),
             in_specs=[
                 pl.BlockSpec((nb, rows), lambda g, p: (0, 0)),
-                pl.BlockSpec((senders, 3, per, width), lambda g, p: (0, 0, jnp.minimum(g, nb - 1), 0)),
+                *[
+                    pl.BlockSpec(
+                        (senders, per, width),
+                        lambda g, p, i=i: (0, i * nb + jnp.minimum(g, nb - 1), 0),
+                    )
+                    for i in range(3)
+                ],
             ],
             out_specs=pl.BlockSpec((senders, per, width), lambda g, p: (0, jnp.maximum(g - lag, 0), 0)),
             scratch_shapes=[
                 pltpu.VMEM((total, width), jnp.bfloat16),
                 pltpu.VMEM((total, 2 * width), jnp.bfloat16),
                 pltpu.VMEM((2, rows, width), jnp.bfloat16),
-                pltpu.VMEM((2, 1, rows), jnp.int32),
             ],
         ),
         out_shape=jax.ShapeDtypeStruct((senders, nb * per, width), jnp.bfloat16),
-    )(pattern, members, arrived)
+    )(pattern, slots, arrived, arrived, arrived)
 
 
 def unpack(order, returned):
@@ -339,53 +376,74 @@
     count = lax.axis_size("seq")
     line = count // 4
     me = lax.axis_index("seq")
-    right = [(i, i + 4) for i in range(count - 4)]
-    left = [(i + 4, i) for i in range(count - 4)]
+    moves = {
+        "right": [(i, i + 4) for i in range(count - 4)],
+        "left": [(i + 4, i) for i in range(count - 4)],
+        "x": [(i, i ^ 1) for i in range(count)],
+        "y": [(i, i ^ 2) for i in range(count)],
+    }
+
+    def moved(cells, way):
+        return lax.ppermute(cells, "seq", moves[way])
+
+    half = w_out.shape[0] // 2
+    own = (w_out[None, :half], w_out[None, half:])
     from_left, from_right = [w_out], [w_out]
-    for _ in range(line - 1):
-        from_left.append(lax.ppermute(from_left[-1], "seq", right))
-        from_right.append(lax.ppermute(from_right[-1], "seq", left))
-    stack = [w_out] + [from_left[k] + from_right[line - k] for k in range(1, line)]
-    half = w_out.shape[0] // 2
-
-    def doubled(cells, bit):
-        other = lax.ppermute(cells, "seq", [(i, i ^ bit) for i in range(count)])
-        return jnp.concatenate([cells, other], axis=0)
-
-    first = doubled(doubled(jnp.stack([cell[:half] for cell in stack]), 2), 1)
-    second = doubled(doubled(jnp.stack([cell[half:] for cell in stack]), 1), 2)
+    from_left.append(moved(w_out, "right"))
+    from_right.append(moved(w_out, "left"))
+    ways = (("y", "x"), ("x", "y"))
+
+    def spread(cells):
+        both = []
+        for color in range(2):
+            there = moved(cells[color], ways[color][0])
+            two = jnp.concatenate([cells[color], there], axis=0)
+            both.append((two, moved(two, ways[color][1])))
+        return both
+
+    near = spread(own)
+    for _ in range(2, line):
+        from_left.append(moved(from_left[-1], "right"))
+        from_right.append(moved(from_right[-1], "left"))
+    rest = [from_left[k] + from_right[line - k] for k in range(1, line)]
+    far = spread(
+        (jnp.stack([cell[:half] for cell in rest]), jnp.stack([cell[half:] for cell in rest]))
+    )
+    stacks = [jnp.concatenate([*near[color], *far[color]], axis=0) for color in range(2)]
     names = jnp.arange(count, dtype=jnp.int32)
     step = jnp.mod(me // 4 - names // 4, line)
     differ = jnp.bitwise_xor(me, names)
-    low, high = differ % 2, (differ // 2) % 2
-    return first, second, (low * 2 + high) * line + step, (high * 2 + low) * line + step
+    x_bit, y_bit = differ % 2, (differ // 2) % 2
+
+    def place(inner, outer):
+        return jnp.where(
+            step == 0,
+            outer * 2 + inner,
+            4 + (outer * 2 + inner) * (line - 1) + step - 1,
+        )
+
+    return stacks, (place(y_bit, x_bit), place(x_bit, y_bit)), from_left[2]
 
 
 def head_shards(queries, keys, values, route, members, pattern, w_out):
     heads, rows = route.shape
     count = lax.axis_size("seq")
-    extra = pattern.shape[1] * pattern.shape[2]
-    meta = jnp.concatenate(
-        [
-            members,
-            pattern.reshape(heads, extra),
-            jnp.zeros((heads, LANES - extra), jnp.int32),
-        ],
-        axis=1,
-    )
-    meta = lax.all_to_all(meta, "seq", split_axis=0, concat_axis=0, tiled=True)
-    packed, order = pack(route, queries, keys, values)
+    entries = pattern.shape[1] * pattern.shape[2]
+    pattern = jnp.pad(pattern.reshape(heads, entries), ((0, 0), (0, LANES - entries)))
+    stacks, places, hop = gather_weights(w_out)
+    packed, order = pack(route, pattern, queries, keys, values)
+    packed, _ = lax.optimization_barrier((packed, hop))
     arrived = lax.all_to_all(packed, "seq", split_axis=0, concat_axis=0, tiled=True)
-    first, second, at_first, at_second = gather_weights(w_out)
-    context = attend(meta[:, :rows], meta[:, rows : rows + extra].reshape(-1), arrived)
+    slots, pattern = tail_of(arrived, rows, entries)
+    context = attend(slots, pattern, arrived)
     returned = lax.all_to_all(context, "seq", split_axis=0, concat_axis=0, tiled=True)
     attended = unpack(order, returned)
     mine = lax.axis_index("tp")
     half = count // 2
 
     def part(which):
-        places = [lax.dynamic_slice_in_dim(at, which * half, half) for at in (at_first, at_second)]
-        return project(places[0], places[1], attended, first, second)
+        at = [lax.dynamic_slice_in_dim(place, which * half, half) for place in places]
+        return project(at[0], at[1], attended, stacks[0], stacks[1])
 
     send = part(1 - mine)
     received = lax.ppermute(send, "tp", [(0, 1), (1, 0)])

time: 457 us -> 513 us (1.12)
  waiting for transfers between devices: 252 us -> 325 us
  starting transfers between devices: 81.1 us -> 44.2 us
  other arithmetic: 5.93 us -> 17.9 us
  local copies, waits for them, and re-layouts: 24.9 us -> 34.1 us
    ppermute x10 -> x14, waiting for transfers between devices: 252 us -> 325 us  [moved(): return lax.ppermute(cells, 'seq', moves[way])]
    ppermute x10 -> x14, starting transfers between devices: 60 us -> 30 us  [moved(): return lax.ppermute(cells, 'seq', moves[way])]
    unnamed x10 -> x35, local copies, waits for them, and re-layouts: 7.86 us -> 21.4 us
    all_to_all x1 -> x0, starting transfers between devices: 8.34 us -> none  [head_shards(): meta = lax.all_to_all(meta, 'seq', split_axis=0, concat_axis=0, tiled=True)]
    concatenate x1 -> x4, other arithmetic: 0.76 us -> 8.31 us  [spread(): two = jnp.concatenate([cells[color], there], axis=0)]
    concatenate x5 -> x2, local copies, waits for them, and re-layouts: 13.5 us -> 7.52 us  [gather_weights(): jnp.concatenate([*near[color], *far[color]], axis=0)]
  transfers between devices with their start and end apart: 14 -> 17, of which waited for: 6 -> 10; matrix products, arithmetic and copies ran while one was open for 5% -> 9% of each run, Pallas kernels for 15% -> 13%
where the time goes in v2:
time: 513 us; the launch traced here: 511 us
  waiting for transfers between devices  325 us (63%)
  Pallas kernels  89.6 us (17%)
  starting transfers between devices  44.2 us (9%)
  local copies, waits for them, and re-layouts  34.1 us (7%)
  other arithmetic  17.9 us (3%)
    ppermute x14, waiting for transfers between devices, moved(): return lax.ppermute(cells, 'seq', moves[way])  325 us
    pallas_call x1, Pallas kernels, attend(): pl.pallas_call(kernel, name='attend', grid_spec=pltpu.PrefetchScalarGridS...  36.9 us
    ppermute x14, starting transfers between devices, moved(): return lax.ppermute(cells, 'seq', moves[way])  30 us
    pallas_call x2, Pallas kernels, project(): pl.pallas_call(kernel, name='project', grid_spec=pltpu.PrefetchScalarGrid...  22.3 us
    unnamed x35, local copies, waits for them, and re-layouts  21.4 us
    pallas_call x1, Pallas kernels, pack(): pl.pallas_call(kernel, name='pack', grid=(heads,), in_specs=[pl.BlockSpec...  18.7 us
    pallas_call x1, Pallas kernels, unpack(): pl.pallas_call(kernel, name='unpack', grid=(heads,), in_specs=[pl.BlockSp...  11.8 us
  transfers between devices with their start and end apart: 17, of which 10 were waited for; matrix products, arithmetic and copies ran while one was open for 9% of the time, Pallas kernels for 13%

profile of v2, /device:TPU:0, one launch (start us, length us, event | category | flops | bytes accessed | tf_op | source)
XLA Modules:
  0.0 510.7 jit_solution(713399589485616524)
XLA Ops:
  0.0 5.0 collective-permute-start
  5.0 22.6 %collective-permute-done = bf16[2048,256]{1,0:T(8,128)(2,1)S(1)} collective-permute-done((bf16[2048,256]{1,0:T(8,128)(2,1)}, bf16[2048,256]{1,0:T(8,128)(2,1)S(1)}, u32[]{:S(2)}, u32[]{:S(2)}) %collective-permute-start) | collective-permute-done | bytes 1048608 | tf_op jit(solution)/shard_map/ppermute | solution.py:387
  27.7 5.3 %collective-permute-start.1 = (bf16[2048,256]{1,0:T(8,128)(2,1)S(1)}, bf16[2048,256]{1,0:T(8,128)(2,1)}, u32[]{:S(2)}, u32[]{:S(2)}) collective-permute-start(bf16[2048,256]{1,0:T(8,128)(2,1)S(1)} %collective-permute-done), channel_id=1, source_target_pairs={{0,8},{2,10},{4,12},{6,14},{8,16},{10,18},{12,20},{14,22},{16,24},... | collective-permute-start | bytes 3145736 | tf_op jit(solution)/shard_map/ppermute | solution.py:387
  34.4 18.7 %pack.1 = (bf16[16,1568,128]{2,1,0:T(8,128)(2,1)}, s32[16,1,512]{2,1,0:T(1,128)}) custom-call(s32[16,512]{1,0:T(8,128)} %route_ref.1, s32[16,128]{1,0:T(8,128)} %pad.4.pat_ref, bf16[512,2048]{1,0:T(8,128)(2,1)} %q_ref.1, bf16[512,2048]{1,0:T(8,128)(2,1)} %k_ref.1, bf16[512,2048]{1,0:T(8,128)(2,1)} %v_ref.1), custom_call_target="tpu_custom_call" | custom-call | tf_op jit(solution)/shard_map/pack/pallas_call | solution.py:205
  53.5 8.1 %all-to-all-start = ((bf16[16,1568,128]{2,1,0:T(8,128)(2,1)}), bf16[16,1568,128]{2,1,0:T(8,128)(2,1)}, u32[]{:S(2)}, u32[]{:S(2)}) async-start(bf16[16,1568,128]{2,1,0:T(8,128)(2,1)} %get-tuple-element.10), calls=%async_computation | async-start | bytes 12845056 | tf_op jit(solution)/shard_map/all_to_all | solution.py:436
  62.9 124.9 %collective-permute-done.4 = bf16[2048,256]{1,0:T(8,128)(2,1)S(1)} collective-permute-done((bf16[2048,256]{1,0:T(8,128)(2,1)S(1)}, bf16[2048,256]{1,0:T(8,128)(2,1)S(1)}, u32[]{:S(2)}, u32[]{:S(2)}) %collective-permute-start.4) | collective-permute-done | bytes 1048608 | tf_op jit(solution)/shard_map/ppermute | solution.py:387
  189.0 59.0 %collective-permute-done.5 = bf16[2048,256]{1,0:T(8,128)(2,1)S(1)} collective-permute-done((bf16[2048,256]{1,0:T(8,128)(2,1)S(1)}, bf16[2048,256]{1,0:T(8,128)(2,1)S(1)}, u32[]{:S(2)}, u32[]{:S(2)}) %collective-permute-start.5) | collective-permute-done | bytes 1048608 | tf_op jit(solution)/shard_map/ppermute | solution.py:387
  249.4 4.6 collective-permute-start.7
  255.6 18.0 %collective-permute-done.6 = bf16[2048,256]{1,0:T(8,128)(2,1)S(1)} collective-permute-done((bf16[2048,256]{1,0:T(8,128)(2,1)S(1)}, bf16[2048,256]{1,0:T(8,128)(2,1)S(1)}, u32[]{:S(2)}, u32[]{:S(2)}) %collective-permute-start.6) | collective-permute-done | bytes 1048608 | tf_op jit(solution)/shard_map/ppermute | solution.py:387
  277.0 2.7 collective-permute-start.12
  284.9 36.9 %attend.1 = bf16[16,512,128]{2,1,0:T(8,128)(2,1)} custom-call(s32[320]{0:T(512)} %reshape_squeeze.3.pat_ref, s32[16,512]{1,0:T(8,128)} %reshape.11.slot_ref, bf16[16,1568,128]{2,1,0:T(8,128)(2,1)} %all-to-all-done.q_ref.k_ref.v_ref, bf16[16,1568,128]{2,1,0:T(8,128)(2,1)} %all-to-all-done.q_ref.k_ref.v_ref, bf16[16,1568,128]{2,1,0:T(8,128)(2,1)} %all-to-all-done.q_ref.k_ref.v_ref), custom_call_target="tpu_custom_call" | custom-call | tf_op jit(solution)/shard_map/attend/pallas_call | solution.py:302
  321.8 6.2 %all-to-all-start.1 = ((bf16[16,512,128]{2,1,0:T(8,128)(2,1)}), bf16[16,512,128]{2,1,0:T(8,128)(2,1)}, u32[]{:S(2)}, u32[]{:S(2)}) async-start(bf16[16,512,128]{2,1,0:T(8,128)(2,1)} %attend.1), calls=%async_computation.1 | async-start | bytes 4194304 | tf_op jit(solution)/shard_map/all_to_all | solution.py:439
  329.4 1.9 collective-permute-start.10
  331.3 3.2 pad_maximum_fusion.1
  335.9 3.0 pad_maximum_fusion
  339.6 20.0 %collective-permute-done.10 = bf16[1,1024,256]{2,1,0:T(8,128)(2,1)S(1)} collective-permute-done((bf16[1,1024,256]{2,1,0:T(8,128)(2,1)S(1)}, bf16[1,1024,256]{2,1,0:T(8,128)(2,1)S(1)}, u32[]{:S(2)}, u32[]{:S(2)}) %collective-permute-start.10) | collective-permute-done | bytes 524320 | tf_op jit(solution)/shard_map/ppermute | solution.py:387
  363.0 66.1 %collective-permute-done.2 = bf16[1,1024,256]{2,1,0:T(8,128)(2,1)S(1)} collective-permute-done((bf16[1,1024,256]{2,1,0:T(8,128)(2,1)S(1)}, bf16[1,1024,256]{2,1,0:T(8,128)(2,1)S(1)}, u32[]{:S(2)}, u32[]{:S(2)}) %collective-permute-start.2) | collective-permute-done | bytes 524320 | tf_op jit(solution)/shard_map/ppermute | solution.py:387
  433.9 2.2 constant_dynamic-update-slice_fusion.15
  436.1 1.9 constant_dynamic-update-slice_fusion.14
  438.0 1.9 constant_dynamic-update-slice_fusion.6
  439.9 10.7 %collective-permute-done.11 = bf16[2,1024,256]{2,1,0:T(8,128)(2,1)} collective-permute-done((bf16[2,1024,256]{2,1,0:T(8,128)(2,1)}, bf16[2,1024,256]{2,1,0:T(8,128)(2,1)}, u32[]{:S(2)}, u32[]{:S(2)}) %collective-permute-start.11) | collective-permute-done | bytes 1048608 | tf_op jit(solution)/shard_map/ppermute | solution.py:387
  450.6 2.3 constant_dynamic-update-slice_fusion.13
  452.8 1.7 collective-permute-done.3
  454.6 2.3 constant_dynamic-update-slice_fusion.5
  460.0 2.7 constant_dynamic-update-slice_fusion.9
  462.6 2.7 constant_dynamic-update-slice_fusion.1
  465.3 3.7 constant_dynamic-update-slice_fusion.8.s_ref
  469.0 3.8 constant_dynamic-update-slice_fusion.f_ref
  472.8 11.8 %unpack.1.a_ref = bf16[512,2048]{1,0:T(8,128)(2,1)} custom-call(s32[16,1,512]{2,1,0:T(1,128)} %get-tuple-element.8.order_ref, bf16[16,512,128]{2,1,0:T(8,128)(2,1)} %all-to-all-done.1.in_ref), custom_call_target="tpu_custom_call" | custom-call | tf_op jit(solution)/shard_map/unpack/pallas_call | solution.py:335
  484.6 11.1 %project.3 = bf16[512,2048]{1,0:T(8,128)(2,1)} custom-call(s32[8]{0:T(128)} %get-tuple-element.30.at_ref, s32[8]{0:T(128)} %get-tuple-element.28.too_ref, bf16[512,2048]{1,0:T(8,128)(2,1)} %unpack.1.a_ref, bf16[16,1024,256]{2,1,0:T(8,128)(2,1)} %constant_dynamic-update-slice_fusion.f_ref, bf16[16,1024,256]{2,1,0:T(8,128)(2,1)} %constant_dynamic-update-slice_fusion.8.s_ref), custom_call_target="tpu_custom_call" | custom-call | tf_op jit(solution)/shard_map/project/pallas_call | solution.py:358
  495.8 11.1 %project.2 = bf16[512,2048]{1,0:T(8,128)(2,1)} custom-call(s32[8]{0:T(128)} %get-tuple-element.29.at_ref, s32[8]{0:T(128)} %get-tuple-element.27.too_ref, bf16[512,2048]{1,0:T(8,128)(2,1)} %unpack.1.a_ref, bf16[16,1024,256]{2,1,0:T(8,128)(2,1)} %constant_dynamic-update-slice_fusion.f_ref, bf16[16,1024,256]{2,1,0:T(8,128)(2,1)} %constant_dynamic-update-slice_fusion.8.s_ref), custom_call_target="tpu_custom_call" | custom-call | tf_op jit(solution)/shard_map/project/pallas_call | solution.py:358
  506.9 3.8 add_convert_fusion
  (70 shorter events, 30.7 us)
Async XLA Ops:
  0.0 27.7 %collective-permute-start = (bf16[2048,256]{1,0:T(8,128)(2,1)}, bf16[2048,256]{1,0:T(8,128)(2,1)S(1)}, u32[]{:S(2)}, u32[]{:S(2)}) collective-permute-start(bf16[2048,256]{1,0:T(8,128)(2,1)} %param.12), channel_id=1, source_target_pairs={{0,8},{2,10},{4,12},{6,14},{8,16},{10,18},{12,20},{14,22},{16,24},... | collective-permute-start | bytes 3145736 | tf_op jit(solution)/shard_map/ppermute | solution.py:387
  27.7 25.8 %collective-permute-start.1 = (bf16[2048,256]{1,0:T(8,128)(2,1)S(1)}, bf16[2048,256]{1,0:T(8,128)(2,1)}, u32[]{:S(2)}, u32[]{:S(2)}) collective-permute-start(bf16[2048,256]{1,0:T(8,128)(2,1)S(1)} %collective-permute-done), channel_id=1, source_target_pairs={{0,8},{2,10},{4,12},{6,14},{8,16},{10,18},{12,20},{14,22},{16,24},... | collective-permute-start | bytes 3145736 | tf_op jit(solution)/shard_map/ppermute | solution.py:387
  53.5 8.1 %copy-start.9 = (bf16[2048,256]{1,0:T(8,128)(2,1)S(1)}, bf16[2048,256]{1,0:T(8,128)(2,1)}, u32[]{:S(2)}) copy-start(bf16[2048,256]{1,0:T(8,128)(2,1)} %param.12) | copy-start | bytes 3145732
  53.5 228.9 %all-to-all-start = ((bf16[16,1568,128]{2,1,0:T(8,128)(2,1)}), bf16[16,1568,128]{2,1,0:T(8,128)(2,1)}, u32[]{:S(2)}, u32[]{:S(2)}) async-start(bf16[16,1568,128]{2,1,0:T(8,128)(2,1)} %get-tuple-element.10), calls=%async_computation | async-start | bytes 12845056 | tf_op jit(solution)/shard_map/all_to_all | solution.py:436
  61.6 126.2 %collective-permute-start.4 = (bf16[2048,256]{1,0:T(8,128)(2,1)S(1)}, bf16[2048,256]{1,0:T(8,128)(2,1)S(1)}, u32[]{:S(2)}, u32[]{:S(2)}) collective-permute-start(bf16[2048,256]{1,0:T(8,128)(2,1)S(1)} %copy-done.9), channel_id=1, source_target_pairs={{8,0},{10,2},{12,4},{14,6},{16,8},{18,10},{20,12},{22,14},{24,16},... | collective-permute-start | bytes 3145736 | tf_op jit(solution)/shard_map/ppermute | solution.py:387
  187.8 60.3 %collective-permute-start.5 = (bf16[2048,256]{1,0:T(8,128)(2,1)S(1)}, bf16[2048,256]{1,0:T(8,128)(2,1)S(1)}, u32[]{:S(2)}, u32[]{:S(2)}) collective-permute-start(bf16[2048,256]{1,0:T(8,128)(2,1)S(1)} %collective-permute-done.4), channel_id=1, source_target_pairs={{8,0},{10,2},{12,4},{14,6},{16,8},{18,10},{20,12},{22,14},{24,16},... | collective-permute-start | bytes 3145736 | tf_op jit(solution)/shard_map/ppermute | solution.py:387
  248.1 25.5 %collective-permute-start.6 = (bf16[2048,256]{1,0:T(8,128)(2,1)S(1)}, bf16[2048,256]{1,0:T(8,128)(2,1)S(1)}, u32[]{:S(2)}, u32[]{:S(2)}) collective-permute-start(bf16[2048,256]{1,0:T(8,128)(2,1)S(1)} %collective-permute-done.5), channel_id=1, source_target_pairs={{8,0},{10,2},{12,4},{14,6},{16,8},{18,10},{20,12},{22,14},{24,16},... | collective-permute-start | bytes 3145736 | tf_op jit(solution)/shard_map/ppermute | solution.py:387
  249.4 25.7 %collective-permute-start.7 = (bf16[2048,256]{1,0:T(8,128)(2,1)}, bf16[2048,256]{1,0:T(8,128)(2,1)S(1)}, u32[]{:S(2)}, u32[]{:S(2)}) collective-permute-start(bf16[2048,256]{1,0:T(8,128)(2,1)} %collective-permute-done.1), channel_id=1, source_target_pairs={{0,8},{2,10},{4,12},{6,14},{8,16},{10,18},{12,20},{14,22},{16,24},... | collective-permute-start | bytes 3145736 | tf_op jit(solution)/shard_map/ppermute | solution.py:387
  255.6 20.0 %copy-start.2 = (bf16[1,1024,256]{2,1,0:T(8,128)(2,1)}, bf16[1,1024,256]{2,1,0:T(8,128)(2,1)S(1)}, u32[]{:S(2)}) copy-start(bf16[1,1024,256]{2,1,0:T(8,128)(2,1)S(1)} %get-tuple-element.13) | copy-start | bytes 1572868
  255.6 24.1 %copy-start = (bf16[1,1024,256]{2,1,0:T(8,128)(2,1)}, bf16[1,1024,256]{2,1,0:T(8,128)(2,1)S(1)}, u32[]{:S(2)}) copy-start(bf16[1,1024,256]{2,1,0:T(8,128)(2,1)S(1)} %get-tuple-element.14) | copy-start | bytes 1572868
  275.4 5.6 %copy-start.3 = (bf16[1,1024,256]{2,1,0:T(8,128)(2,1)}, bf16[1,1024,256]{2,1,0:T(8,128)(2,1)S(1)}, u32[]{:S(2)}) copy-start(bf16[1,1024,256]{2,1,0:T(8,128)(2,1)S(1)} %get-tuple-element.16) | copy-start | bytes 1572868
  275.4 5.6 %copy-start.7 = (bf16[1,1024,256]{2,1,0:T(8,128)(2,1)}, bf16[1,1024,256]{2,1,0:T(8,128)(2,1)S(1)}, u32[]{:S(2)}) copy-start(bf16[1,1024,256]{2,1,0:T(8,128)(2,1)S(1)} %get-tuple-element.15) | copy-start | bytes 1572868
  275.5 5.5 %copy-start.5 = (bf16[1,1024,256]{2,1,0:T(8,128)(2,1)}, bf16[1,1024,256]{2,1,0:T(8,128)(2,1)S(1)}, u32[]{:S(2)}) copy-start(bf16[1,1024,256]{2,1,0:T(8,128)(2,1)S(1)} %get-tuple-element.12) | copy-start | bytes 1572868
  275.5 5.5 %copy-start.8 = (bf16[1,1024,256]{2,1,0:T(8,128)(2,1)}, bf16[1,1024,256]{2,1,0:T(8,128)(2,1)S(1)}, u32[]{:S(2)}) copy-start(bf16[1,1024,256]{2,1,0:T(8,128)(2,1)S(1)} %get-tuple-element.11) | copy-start | bytes 1572868
  277.0 54.2 %collective-permute-start.12 = (bf16[3,1024,256]{2,1,0:T(8,128)(2,1)}, bf16[3,1024,256]{2,1,0:T(8,128)(2,1)}, u32[]{:S(2)}, u32[]{:S(2)}) collective-permute-start(bf16[3,1024,256]{2,1,0:T(8,128)(2,1)} %pad_maximum_fusion.3), channel_id=1, source_target_pairs={{0,2},{2,0},{4,6},{6,4},{8,10},{10,8},{12,14},{14,12},{16,18},{18,... | collective-permute-start | bytes 4718600 | tf_op jit(solution)/shard_map/ppermute | solution.py:387
  281.0 54.9 %collective-permute-start.8 = (bf16[3,1024,256]{2,1,0:T(8,128)(2,1)}, bf16[3,1024,256]{2,1,0:T(8,128)(2,1)}, u32[]{:S(2)}, u32[]{:S(2)}) collective-permute-start(bf16[3,1024,256]{2,1,0:T(8,128)(2,1)} %pad_maximum_fusion.2), channel_id=1, source_target_pairs={{0,4},{2,6},{4,0},{6,2},{8,12},{10,14},{12,8},{14,10},{16,20},{18,... | collective-permute-start | bytes 4718600 | tf_op jit(solution)/shard_map/ppermute | solution.py:387
  321.8 151.1 %all-to-all-start.1 = ((bf16[16,512,128]{2,1,0:T(8,128)(2,1)}), bf16[16,512,128]{2,1,0:T(8,128)(2,1)}, u32[]{:S(2)}, u32[]{:S(2)}) async-start(bf16[16,512,128]{2,1,0:T(8,128)(2,1)} %attend.1), calls=%async_computation.1 | async-start | bytes 4194304 | tf_op jit(solution)/shard_map/all_to_all | solution.py:439
  327.9 8.0 %copy-start.1 = (bf16[1,1024,256]{2,1,0:T(8,128)(2,1)S(1)}, bf16[1,1024,256]{2,1,0:T(8,128)(2,1)}, u32[]{:S(2)}) copy-start(bf16[1,1024,256]{2,1,0:T(8,128)(2,1)} %copy-done) | copy-start | bytes 1572868
  327.9 8.0 %copy-start.4 = (bf16[1,1024,256]{2,1,0:T(8,128)(2,1)S(1)}, bf16[1,1024,256]{2,1,0:T(8,128)(2,1)}, u32[]{:S(2)}) copy-start(bf16[1,1024,256]{2,1,0:T(8,128)(2,1)} %copy-done.3) | copy-start | bytes 1572868
  328.0 8.0 %copy-start.6 = (bf16[1,1024,256]{2,1,0:T(8,128)(2,1)S(1)}, bf16[1,1024,256]{2,1,0:T(8,128)(2,1)}, u32[]{:S(2)}) copy-start(bf16[1,1024,256]{2,1,0:T(8,128)(2,1)} %copy-done.5) | copy-start | bytes 1572868
  329.4 30.3 %collective-permute-start.10 = (bf16[1,1024,256]{2,1,0:T(8,128)(2,1)S(1)}, bf16[1,1024,256]{2,1,0:T(8,128)(2,1)S(1)}, u32[]{:S(2)}, u32[]{:S(2)}) collective-permute-start(bf16[1,1024,256]{2,1,0:T(8,128)(2,1)S(1)} %get-tuple-element.23), channel_id=1, source_target_pairs={{0,2},{2,0},{4,6},{6,4},{8,10},{10,8},{12,14},{14,12},{16,18},{18,... | collective-permute-start | bytes 1572872 | tf_op jit(solution)/shard_map/ppermute | solution.py:387
  334.4 130.9 %collective-permute-start.13 = (bf16[6,1024,256]{2,1,0:T(8,128)(2,1)}, bf16[6,1024,256]{2,1,0:T(8,128)(2,1)}, u32[]{:S(2)}, u32[]{:S(2)}) collective-permute-start(bf16[6,1024,256]{2,1,0:T(8,128)(2,1)} %pad_maximum_fusion.1), channel_id=1, source_target_pairs={{0,4},{2,6},{4,0},{6,2},{8,12},{10,14},{12,8},{14,10},{16,20},{18,... | collective-permute-start | bytes 9437192 | tf_op jit(solution)/shard_map/ppermute | solution.py:387
  338.9 130.1 %collective-permute-start.9 = (bf16[6,1024,256]{2,1,0:T(8,128)(2,1)}, bf16[6,1024,256]{2,1,0:T(8,128)(2,1)}, u32[]{:S(2)}, u32[]{:S(2)}) collective-permute-start(bf16[6,1024,256]{2,1,0:T(8,128)(2,1)} %pad_maximum_fusion), channel_id=1, source_target_pairs={{0,2},{2,0},{4,6},{6,4},{8,10},{10,8},{12,14},{14,12},{16,18},{18,... | collective-permute-start | bytes 9437192 | tf_op jit(solution)/shard_map/ppermute | solution.py:387
  339.5 89.5 %collective-permute-start.2 = (bf16[1,1024,256]{2,1,0:T(8,128)(2,1)S(1)}, bf16[1,1024,256]{2,1,0:T(8,128)(2,1)S(1)}, u32[]{:S(2)}, u32[]{:S(2)}) collective-permute-start(bf16[1,1024,256]{2,1,0:T(8,128)(2,1)S(1)} %get-tuple-element.24), channel_id=1, source_target_pairs={{0,4},{2,6},{4,0},{6,2},{8,12},{10,14},{12,8},{14,10},{16,20},{18,... | collective-permute-start | bytes 1572872 | tf_op jit(solution)/shard_map/ppermute | solution.py:387
  359.6 0.8 copy-start.10
  361.5 89.1 %collective-permute-start.11 = (bf16[2,1024,256]{2,1,0:T(8,128)(2,1)}, bf16[2,1024,256]{2,1,0:T(8,128)(2,1)}, u32[]{:S(2)}, u32[]{:S(2)}) collective-permute-start(bf16[2,1024,256]{2,1,0:T(8,128)(2,1)} %pad_maximum_fusion.5), channel_id=1, source_target_pairs={{0,4},{2,6},{4,0},{6,2},{8,12},{10,14},{12,8},{14,10},{16,20},{18,... | collective-permute-start | bytes 3145736 | tf_op jit(solution)/shard_map/ppermute | solution.py:387
  429.0 0.8 copy-start.11
  430.9 23.6 %collective-permute-start.3 = (bf16[2,1024,256]{2,1,0:T(8,128)(2,1)}, bf16[2,1024,256]{2,1,0:T(8,128)(2,1)}, u32[]{:S(2)}, u32[]{:S(2)}) collective-permute-start(bf16[2,1024,256]{2,1,0:T(8,128)(2,1)} %pad_maximum_fusion.4), channel_id=1, source_target_pairs={{0,2},{2,0},{4,6},{6,4},{8,10},{10,8},{12,14},{14,12},{16,18},{18,... | collective-permute-start | bytes 3145736 | tf_op jit(solution)/shard_map/ppermute | solution.py:387
  495.8 11.1 %collective-permute-start.14 = (bf16[512,2048]{1,0:T(8,128)(2,1)}, bf16[512,2048]{1,0:T(8,128)(2,1)S(1)}, u32[]{:S(2)}, u32[]{:S(2)}) collective-permute-start(bf16[512,2048]{1,0:T(8,128)(2,1)} %project.3), channel_id=1, source_target_pairs={{0,1},{1,0},{2,3},{3,2},{4,5},{5,4},{6,7},{7,6},{8,9},{9,8},{10,11... | collective-permute-start | bytes 6291464 | tf_op jit(solution)/shard_map/ppermute | solution.py:449

commit v3 on v2

--- a/solution.py
+++ b/solution.py
@@ -149,63 +149,90 @@
     return jnp.concatenate(counts, axis=1)
 
 
-def table_to(order_row):
+def table_to(order_row, first, last):
     n = order_row.shape[1]
-    rows = lax.broadcasted_iota(jnp.int32, (n, n), 0)
+    rows = lax.broadcasted_iota(jnp.int32, (last - first, n), 0) + first
     return jnp.where(rows == order_row, 1.0, 0.0).astype(jnp.bfloat16)
 
 
-def table_from(order_row):
+def table_from(order_row, first, last):
     n = order_row.shape[1]
     order_col = jnp.broadcast_to(order_row, (LANES, n)).T
-    lane = lax.broadcasted_iota(jnp.int32, (n, LANES), 1)
-    parts = [
-        jnp.where(order_col == lane + j * LANES, 1.0, 0.0).astype(jnp.bfloat16)
-        for j in range(n // LANES)
-    ]
-    return jnp.concatenate(parts, axis=1)
+    parts = []
+    for start in range(first, last, LANES):
+        lane = lax.broadcasted_iota(jnp.int32, (n, min(LANES, last - start)), 1) + start
+        parts.append(jnp.where(order_col[:, : lane.shape[1]] == lane, 1.0, 0.0).astype(jnp.bfloat16))
+    return jnp.concatenate(parts, axis=1) if len(parts) > 1 else parts[0]
 
 
 def mm(a, b):
     return jnp.dot(a, b, preferred_element_type=jnp.float32)
 
 
-def pack(route, pattern, queries, keys, values):
+def pack(route, pattern, queries, keys, values, first, last, order=None):
     heads, rows = route.shape
     width = queries.shape[1] // heads
     lines = rows // LANES
-
-    def kernel(route_ref, pat_ref, q_ref, k_ref, v_ref, out_ref, order_ref):
-        h = pl.program_id(0)
-        row = route_ref[pl.ds(h, 1), :]
-        order = order_of(row)
-        order_ref[0] = order
-        table = table_to(order)
-        out_ref[0, 0:rows] = mm(table, q_ref[...]).astype(jnp.bfloat16)
-        out_ref[0, rows : 2 * rows] = mm(table, k_ref[...]).astype(jnp.bfloat16)
-        out_ref[0, 2 * rows : 3 * rows] = mm(table, v_ref[...]).astype(jnp.bfloat16)
-        slot = jnp.bitwise_and(row, rows - 1)
-        high = lax.shift_right_logical(slot, DIGIT)
-        low = jnp.bitwise_and(slot, (1 << DIGIT) - 1)
-        at = lax.broadcasted_iota(jnp.int32, (8, rows), 0)
-        digits = jnp.where(at == 0, high, jnp.where(at == 1, low, 0))
-        digits = digits.astype(jnp.float32).astype(jnp.bfloat16)
-        sorted_digits = lax.dot_general(
-            digits, table, (((1,), (1,)), ((), ())), preferred_element_type=jnp.float32
-        )
-        parts = [
-            sorted_digits[d : d + 1, j * LANES : (j + 1) * LANES] for d in range(2) for j in range(lines)
-        ]
-        parts.append(pat_ref[pl.ds(h, 1), :].astype(jnp.float32))
-        parts.append(jnp.zeros((TAIL - 2 * lines - 1, LANES), jnp.float32))
-        out_ref[0, 3 * rows :] = jnp.concatenate(parts, axis=0).astype(jnp.bfloat16)
-
-    columns = pl.BlockSpec((rows, width), lambda h: (0, h))
-    total = 3 * rows + TAIL
+    leads = order is None
+    part = last - first
+    group = 2
+
+    def emit(i, order_row, refs, out_ref):
+        stacked = jnp.concatenate([ref[:, i * width : (i + 1) * width] for ref in refs], axis=1)
+        put = mm(table_to(order_row, first, last), stacked).astype(jnp.bfloat16)
+        for n in range(3):
+            out_ref[i, n * part : (n + 1) * part] = put[:, n * width : (n + 1) * width]
+
+    def lead(route_ref, pat_ref, q_ref, k_ref, v_ref, out_ref, order_ref):
+        for i in range(group):
+            h = pl.program_id(0) * group + i
+            row = route_ref[pl.ds(h, 1), :]
+            order_row = order_of(row)
+            order_ref[i] = order_row
+            emit(i, order_row, (q_ref, k_ref, v_ref), out_ref)
+            slot = jnp.bitwise_and(row, rows - 1)
+            high = lax.shift_right_logical(slot, DIGIT)
+            low = jnp.bitwise_and(slot, (1 << DIGIT) - 1)
+            at = lax.broadcasted_iota(jnp.int32, (8, rows), 0)
+            digits = jnp.where(at == 0, high, jnp.where(at == 1, low, 0))
+            digits = digits.astype(jnp.float32).astype(jnp.bfloat16)
+            sorted_digits = lax.dot_general(
+                digits,
+                table_to(order_row, 0, rows),
+                (((1,), (1,)), ((), ())),
+                preferred_element_type=jnp.float32,
+            )
+            parts = [
+                sorted_digits[d : d + 1, j * LANES : (j + 1) * LANES]
+                for d in range(2)
+                for j in range(lines)
+            ]
+            parts.append(pat_ref[pl.ds(h, 1), :].astype(jnp.float32))
+            parts.append(jnp.zeros((TAIL - 2 * lines - 1, LANES), jnp.float32))
+            out_ref[i, 3 * part :] = jnp.concatenate(parts, axis=0).astype(jnp.bfloat16)
+
+    def follow(order_ref, q_ref, k_ref, v_ref, out_ref):
+        for i in range(group):
+            emit(i, order_ref[i], (q_ref, k_ref, v_ref), out_ref)
+
+    columns = pl.BlockSpec((rows, group * width), lambda h: (0, h))
+    order_spec = pl.BlockSpec((group, 1, rows), lambda h: (h, 0, 0))
+    total = 3 * part + (TAIL if leads else 0)
+    out_spec = pl.BlockSpec((group, total, width), lambda h: (h, 0, 0))
+    out_shape = jax.ShapeDtypeStruct((heads, total, width), jnp.bfloat16)
+    if not leads:
+        return pl.pallas_call(
+            follow,
+            name="pack_rest",
+            grid=(heads // group,),
+            in_specs=[order_spec, columns, columns, columns],
+            out_specs=out_spec,
+            out_shape=out_shape,
+        )(order, queries, keys, values)
     return pl.pallas_call(
-        kernel,
+        lead,
         name="pack",
-        grid=(heads,),
+        grid=(heads // group,),
         in_specs=[
             pl.BlockSpec((heads, rows), lambda h: (0, 0)),
             pl.BlockSpec((heads, LANES), lambda h: (0, 0)),
@@ -213,68 +240,86 @@
             columns,
             columns,
         ],
-        out_specs=[
-            pl.BlockSpec((1, total, width), lambda h: (h, 0, 0)),
-            pl.BlockSpec((1, 1, rows), lambda h: (h, 0, 0)),
-        ],
-        out_shape=[
-            jax.ShapeDtypeStruct((heads, total, width), jnp.bfloat16),
-            jax.ShapeDtypeStruct((heads, 1, rows), jnp.int32),
-        ],
+        out_specs=[out_spec, order_spec],
+        out_shape=[out_shape, jax.ShapeDtypeStruct((heads, 1, rows), jnp.int32)],
     )(route, pattern, queries, keys, values)
 
 
 def tail_of(arrived, rows, entries):
     senders = arrived.shape[0]
     lines = rows // LANES
-    tail = arrived[:, 3 * rows : 3 * rows + 2 * lines + 1].astype(jnp.int32)
+    tail = arrived[:, -TAIL:].astype(jnp.int32)
     slot = (tail[:, :lines] << DIGIT) + tail[:, lines : 2 * lines]
     slot = slot.reshape(senders, senders, rows // senders).transpose(1, 0, 2)
     return slot.reshape(senders, rows), tail[:, 2 * lines, :entries].reshape(-1)
 
 
-def attend(slots, pattern, arrived):
+def attend(slots, pattern, arrived, count, kept=None):
     nb, rows = slots.shape
     senders, _, width = arrived.shape
     per = rows // senders
     per_block = rows // CLUSTER
     window = (2 * REACH + 1) * CLUSTER
     blocks = window // BLOCK
-    margin = REACH * CLUSTER
-    lag = margin // rows
-    total = nb * rows + 2 * margin
+    leads = kept is None
+    lowest = 0 if leads else nb - count
+    steps = count if leads else count + 1
+    done = count - 1 if leads else count + 1
+    ahead = rows if leads else 2 * rows
+    total = (count + (1 if leads else 3)) * rows
     scale = width ** (-0.5) * 1.4426950408889634
 
-    def kernel(pat_ref, slot_ref, q_ref, k_ref, v_ref, out_ref, kbuf, vbuf, qbuf):
+    def kernel(pat_ref, slot_ref, q_ref, k_ref, v_ref, *refs):
+        if leads:
+            out_ref, q_keep, k_keep, v_keep, kbuf, vbuf, qbuf = refs
+        else:
+            q_kept, k_kept, v_kept, out_ref, kbuf, vbuf, qbuf = refs
         g = pl.program_id(0)
 
         @pl.when(g == 0)
         def _():
-            zero = jnp.zeros((margin, width), jnp.bfloat16)
-            for at in (0, total - margin):
-                kbuf[at : at + margin, :] = zero
-                vbuf[at : at + margin, :width] = zero
+            zero = jnp.zeros((rows, width), jnp.bfloat16)
             vbuf[:, width:] = jnp.ones((total, width), jnp.bfloat16)
-
-        @pl.when(g < nb)
+            if leads:
+                kbuf[:rows, :] = zero
+                vbuf[:rows, :width] = zero
+            else:
+                kbuf[: 2 * rows, :] = k_kept[...]
+                vbuf[: 2 * rows, :width] = v_kept[...]
+                qbuf[(lowest - 1) % 2] = q_kept[...]
+                kbuf[total - rows :, :] = zero
+                vbuf[total - rows :, :width] = zero
+
+        @pl.when(g < count)
         def _():
-            table = table_to(slot_ref[pl.ds(g, 1), :])
-            at = pl.multiple_of(g * rows + margin, rows)
+            block = g + lowest
+            table = table_to(slot_ref[pl.ds(block, 1), :], 0, rows)
+            at = pl.multiple_of(g * rows + ahead, rows)
             put = [
                 mm(table, ref[...].reshape(rows, width)).astype(jnp.bfloat16)
                 for ref in (q_ref, k_ref, v_ref)
             ]
-            qbuf[pl.ds(g % 2, 1)] = put[0][None]
+            qbuf[pl.ds(block % 2, 1)] = put[0][None]
             kbuf[pl.ds(at, rows), :] = put[1]
             vbuf[pl.ds(at, rows), :width] = put[2]
-
-        @pl.when(g >= lag)
+            if leads:
+
+                @pl.when(g == count - 1)
+                def _():
+                    q_keep[...] = put[0]
+                    k_keep[:rows, :] = kbuf[total - 2 * rows : total - rows, :]
+                    v_keep[:rows, :] = vbuf[total - 2 * rows : total - rows, :width]
+                    k_keep[rows:, :] = put[1]
+                    v_keep[rows:, :] = put[2]
+
+        @pl.when(g + lowest > 0)
         def _():
-            b = g - lag
+            b = g + lowest - 1
+            base = (g - 1 if leads else g) * rows
             contexts = []
             for i in range(per_block):
                 q = qbuf[pl.ds(b % 2, 1), i * CLUSTER : (i + 1) * CLUSTER, :][0]
-                at = pl.multiple_of(b * rows + i * CLUSTER, CLUSTER)
+                at = pl.multiple_of(base + i * CLUSTER, CLUSTER)
                 scores = lax.dot_general(
                     q,
                     kbuf[pl.ds(at, window), :],
@@ -296,80 +341,141 @@
                 both = mm(weights, vbuf[pl.ds(at, window), :])
                 contexts.append((both[:, :width] / both[:, width:]).astype(jnp.bfloat16))
             context = jnp.concatenate(contexts, axis=0)
-            back = mm(table_from(slot_ref[pl.ds(b, 1), :]), context).astype(jnp.bfloat16)
+            back = mm(table_from(slot_ref[pl.ds(b, 1), :], 0, rows), context).astype(jnp.bfloat16)
             out_ref[...] = back.reshape(senders, per, width)
 
-    return pl.pallas_call(
+    whole = lambda *shape: pl.BlockSpec(shape, lambda g, p: (0,) * len(shape))
+    incoming = [
+        pl.BlockSpec(
+            (senders, per, width), lambda g, p, i=i: (0, i * count + jnp.minimum(g, count - 1), 0)
+        )
+        for i in range(3)
+    ]
+    keep_specs = [whole(rows, width), whole(2 * rows, width), whole(2 * rows, width)]
+    out_specs = [
+        pl.BlockSpec(
+            (senders, per, width), lambda g, p: (0, jnp.maximum(g - 1, 0) if leads else g, 0)
+        )
+    ]
+    out_shape = [jax.ShapeDtypeStruct((senders, done * per, width), jnp.bfloat16)]
+    if leads:
+        out_specs += keep_specs
+        out_shape += [
+            jax.ShapeDtypeStruct((n * rows, width), jnp.bfloat16) for n in (1, 2, 2)
+        ]
+    out = pl.pallas_call(
         kernel,
-        name="attend",
+        name="attend" if leads else "attend_rest",
         grid_spec=pltpu.PrefetchScalarGridSpec(
             num_scalar_prefetch=1,
-            grid=(nb + lag,),
-            in_specs=[
-                pl.BlockSpec((nb, rows), lambda g, p: (0, 0)),
-                *[
-                    pl.BlockSpec(
-                        (senders, per, width),
-                        lambda g, p, i=i: (0, i * nb + jnp.minimum(g, nb - 1), 0),
-                    )
-                    for i in range(3)
-                ],
-            ],
-            out_specs=pl.BlockSpec((senders, per, width), lambda g, p: (0, jnp.maximum(g - lag, 0), 0)),
+            grid=(steps,),
+            in_specs=[whole(nb, rows), *incoming] + ([] if leads else keep_specs),
+            out_specs=out_specs,
             scratch_shapes=[
                 pltpu.VMEM((total, width), jnp.bfloat16),
                 pltpu.VMEM((total, 2 * width), jnp.bfloat16),
                 pltpu.VMEM((2, rows, width), jnp.bfloat16),
             ],
         ),
-        out_shape=jax.ShapeDtypeStruct((senders, nb * per, width), jnp.bfloat16),
-    )(pattern, slots, arrived, arrived, arrived)
-
-
-def unpack(order, returned):
-    heads, rows, width = returned.shape
-
-    def kernel(order_ref, in_ref, out_ref):
-        out_ref[...] = mm(table_from(order_ref[0]), in_ref[0]).astype(jnp.bfloat16)
-
+        out_shape=out_shape,
+    )(pattern, slots, arrived, arrived, arrived, *(() if leads else kept))
+    return out[0], out[1:]
+
+
+def unpack(order, returned, first, last, partial=None):
+    heads, _, width = returned.shape
+    rows = order.shape[2]
+    group = 4
+
+    def kernel(order_ref, in_ref, *refs):
+        for i in range(group):
+            put = mm(table_from(order_ref[i], first, last), in_ref[i]).astype(jnp.bfloat16)
+            at = slice(i * width, (i + 1) * width)
+            if partial is not None:
+                put = put + refs[0][:, at]
+            refs[-1][:, at] = put
+
+    columns = pl.BlockSpec((rows, group * width), lambda h: (0, h))
     return pl.pallas_call(
         kernel,
-        name="unpack",
-        grid=(heads,),
+        name="unpack" if partial is None else "unpack_rest",
+        grid=(heads // group,),
         in_specs=[
-            pl.BlockSpec((1, 1, rows), lambda h: (h, 0, 0)),
-            pl.BlockSpec((1, rows, width), lambda h: (h, 0, 0)),
-        ],
-        out_specs=pl.BlockSpec((rows, width), lambda h: (0, h)),
+            pl.BlockSpec((group, 1, rows), lambda h: (h, 0, 0)),
+            pl.BlockSpec((group, last - first, width), lambda h: (h, 0, 0)),
+        ]
+        + ([] if partial is None else [columns]),
+        out_specs=columns,
         out_shape=jax.ShapeDtypeStruct((rows, heads * width), jnp.bfloat16),
-    )(order, returned)
-
-
-def project(pieces, pieces_too, attended, first, second):
-    count = pieces.shape[0]
+    )(order, returned, *(() if partial is None else (partial,)))
+
+
+def project(places, attended, cells, received=None, start=0, into=None):
+    count = places.shape[1]
     rows, depth = attended.shape
-    half, cols = first.shape[1:]
-
-    def kernel(at_ref, too_ref, a_ref, f_ref, s_ref, out_ref):
-        out_ref[...] = (mm(a_ref[:, :half], f_ref[0]) + mm(a_ref[:, half:], s_ref[0])).astype(
-            jnp.bfloat16
-        )
-
+    halves, kinds = len(cells), len(cells[0])
+    half, cols = cells[0][0].shape[1:]
+
+    def kernel(at_ref, a_ref, *refs):
+        arrays = [refs[c * kinds : (c + 1) * kinds] for c in range(halves)]
+        rest = refs[halves * kinds :]
+        buffer, sems = rest[-2:]
+        out_ref = rest[-3]
+        j = pl.program_id(0)
+
+        def copy(p, c, source):
+            to = buffer.at[p // 2, pl.ds(c * half, half), pl.ds(p % 2 * cols, cols)]
+            return pltpu.make_async_copy(source, to, sems.at[p, c])
+
+        @pl.when(j == 0)
+        def _():
+            for p in range(count):
+                for c in range(halves):
+                    for kind in range(kinds):
+
+                        @pl.when(at_ref[2 * c, p] == kind)
+                        def _():
+                            copy(p, c, arrays[c][kind].at[at_ref[2 * c + 1, p]]).start()
+
+        for p in range(count):
+
+            @pl.when(j == p // 2)
+            def _():
+                for c in range(halves):
+                    copy(p, c, arrays[c][0].at[0]).wait()
+
+        value = mm(a_ref[...], buffer[pl.ds(j, 1)][0])
+        if received is not None:
+            value = value + rest[0][...].astype(jnp.float32)
+        out_ref[...] = value.astype(jnp.bfloat16)
+
+    anywhere = pl.BlockSpec(memory_space=pl.ANY)
+    in_specs = [pl.BlockSpec((rows, depth), lambda j, at: (0, 0))] + [anywhere] * (halves * kinds)
+    args = [attended] + [cell for group in cells for cell in group]
+    width = count * cols
+    if received is not None:
+        in_specs.append(pl.BlockSpec((rows, 2 * cols), lambda j, at: (0, j)))
+        args.append(received)
+        width = 2 * width
+    if into is not None:
+        in_specs.append(anywhere)
+        args.append(into)
     return pl.pallas_call(
         kernel,
         name="project",
         grid_spec=pltpu.PrefetchScalarGridSpec(
-            num_scalar_prefetch=2,
-            grid=(count,),
-            in_specs=[
-                pl.BlockSpec((rows, depth), lambda j, at, too: (0, 0)),
-                pl.BlockSpec((1, half, cols), lambda j, at, too: (at[j], 0, 0)),
-                pl.BlockSpec((1, half, cols), lambda j, at, too: (too[j], 0, 0)),
+            num_scalar_prefetch=1,
+            grid=(count // 2,),
+            in_specs=in_specs,
+            out_specs=pl.BlockSpec((rows, 2 * cols), lambda j, at: (0, j + start)),
+            scratch_shapes=[
+                pltpu.VMEM((count // 2, depth, 2 * cols), jnp.bfloat16),
+                pltpu.SemaphoreType.DMA((count, halves)),
             ],
-            out_specs=pl.BlockSpec((rows, cols), lambda j, at, too: (0, j)),
         ),
-        out_shape=jax.ShapeDtypeStruct((rows, count * cols), jnp.bfloat16),
-    )(pieces, pieces_too, attended, first, second)
+        out_shape=jax.ShapeDtypeStruct((rows, width), jnp.bfloat16),
+        input_output_aliases={} if into is None else {len(args): 0},
+    )(places, *args)
 
 
 def gather_weights(w_out):
@@ -405,50 +511,66 @@
     for _ in range(2, line):
         from_left.append(moved(from_left[-1], "right"))
         from_right.append(moved(from_right[-1], "left"))
-    rest = [from_left[k] + from_right[line - k] for k in range(1, line)]
-    far = spread(
-        (jnp.stack([cell[:half] for cell in rest]), jnp.stack([cell[half:] for cell in rest]))
-    )
-    stacks = [jnp.concatenate([*near[color], *far[color]], axis=0) for color in range(2)]
+    middle = from_left[2] + from_right[2]
+    middle = [middle[None, :half], middle[None, half:]]
+    mid = spread(middle)
+    ends = [from_left[1] + from_right[3], from_left[3] + from_right[1]]
+    ends = [jnp.stack([cell[at : at + half] for cell in ends]) for at in (0, half)]
+    far = spread(ends)
+    cells = [[*near[c], *mid[c], *far[c]] for c in range(2)]
     names = jnp.arange(count, dtype=jnp.int32)
     step = jnp.mod(me // 4 - names // 4, line)
+    odd = step & 1
+    group = jnp.where(step == 0, 0, 1 + odd)
     differ = jnp.bitwise_xor(me, names)
-    x_bit, y_bit = differ % 2, (differ // 2) % 2
-
-    def place(inner, outer):
-        return jnp.where(
-            step == 0,
-            outer * 2 + inner,
-            4 + (outer * 2 + inner) * (line - 1) + step - 1,
-        )
-
-    return stacks, (place(y_bit, x_bit), place(x_bit, y_bit)), from_left[2]
+    x_bit, y_bit = differ & 1, (differ >> 1) & 1
+    places = []
+    for inner, outer in ((y_bit, x_bit), (x_bit, y_bit)):
+        places.append(outer + 2 * group)
+        places.append(jnp.where(odd == 1, inner * 2 + (step >> 1), inner))
+    return cells, jnp.stack(places)
 
 
 def head_shards(queries, keys, values, route, members, pattern, w_out):
     heads, rows = route.shape
     count = lax.axis_size("seq")
+    per = rows // count
     entries = pattern.shape[1] * pattern.shape[2]
+    early = count // 2
+    cut, cut_back = early * per, (early - 1) * per
     pattern = jnp.pad(pattern.reshape(heads, entries), ((0, 0), (0, LANES - entries)))
-    stacks, places, hop = gather_weights(w_out)
-    packed, order = pack(route, pattern, queries, keys, values)
-    packed, _ = lax.optimization_barrier((packed, hop))
-    arrived = lax.all_to_all(packed, "seq", split_axis=0, concat_axis=0, tiled=True)
+
+    def exchange(cells):
+        return lax.all_to_all(cells, "seq", split_axis=0, concat_axis=0, tiled=True)
+
+    cells, place = gather_weights(w_out)
+    packed, order = pack(route, pattern, queries, keys, values, 0, cut)
+    packed_rest = pack(route, pattern, queries, keys, values, cut, rows, order)
+    arrived = exchange(packed)
+    arrived_rest = exchange(packed_rest)
     slots, pattern = tail_of(arrived, rows, entries)
-    context = attend(slots, pattern, arrived)
-    returned = lax.all_to_all(context, "seq", split_axis=0, concat_axis=0, tiled=True)
-    attended = unpack(order, returned)
+    context, kept = attend(slots, pattern, arrived, early)
+    returned = exchange(context)
+    context_rest, _ = attend(slots, pattern, arrived_rest, count - early, kept)
+    returned_rest = exchange(context_rest)
+    attended = unpack(order, returned, 0, cut_back)
+    attended = unpack(order, returned_rest, cut_back, rows, attended)
     mine = lax.axis_index("tp")
-    half = count // 2
-
-    def part(which):
-        at = [lax.dynamic_slice_in_dim(place, which * half, half) for place in places]
-        return project(at[0], at[1], attended, stacks[0], stacks[1])
-
-    send = part(1 - mine)
-    received = lax.ppermute(send, "tp", [(0, 1), (1, 0)])
-    keep = part(mine)
-    return (keep.astype(jnp.float32) + received.astype(jnp.float32)).astype(jnp.bfloat16)
+    quarter = count // 4
+
+    def places(which, part):
+        return lax.dynamic_slice_in_dim(place, (which * 2 + part) * quarter, quarter, 1)
+
+    received = []
+    for part in range(2):
+        send = project(places(1 - mine, part), attended, cells)
+        received.append(lax.ppermute(send, "tp", [(0, 1), (1, 0)]))
+    mixed = None
+    for part in range(2):
+        mixed = project(
+            places(mine, part), attended, cells, received[part], part * quarter // 2, mixed
+        )
+    return mixed
 
 
 def choose(mesh):
@@ -456,7 +578,7 @@
 
     def shards(queries, keys, values, route, members, pattern, w_out):
         heads, rows = route.shape
-        split = heads == count and groups == 2 and count % 4 == 0
+        split = heads == count and groups == 2 and count == 4 * 4
         tiles = rows == REACH * CLUSTER and queries.shape[1] == heads * LANES
         body = head_shards if split and tiles else slot_shards
         return body(queries, keys, values, route, members, pattern, w_out)

time: 513 us -> 495 us (0.965)
  starting transfers between devices: 44.2 us -> 87.2 us
  waiting for transfers between devices: 325 us -> 285 us
  local copies, waits for them, and re-layouts: 34.1 us -> 8.7 us
  Pallas kernels: 89.6 us -> 97.7 us
    ppermute x14 -> x18, waiting for transfers between devices: 325 us -> 230 us  [moved(): return lax.ppermute(cells, 'seq', moves[way])]
    all_to_all x2 -> x4, waiting for transfers between devices: 0.01 us -> 55 us  [exchange(): return lax.all_to_all(cells, 'seq', split_axis=0, concat_axis=0, tiled=True)]
    ppermute x14 -> x18, starting transfers between devices: 30 us -> 51.6 us  [moved(): return lax.ppermute(cells, 'seq', moves[way])]
    all_to_all x2 -> x4, starting transfers between devices: 14.2 us -> 35 us  [exchange(): return lax.all_to_all(cells, 'seq', split_axis=0, concat_axis=0, tiled=True)]
    unnamed x35 -> x31, local copies, waits for them, and re-layouts: 21.4 us -> 4.69 us
    concatenate x2 -> x0, local copies, waits for them, and re-layouts: 7.52 us -> none  [gather_weights(): jnp.concatenate([*near[color], *far[color]], axis=0)]
    pallas_call x2 -> x4, Pallas kernels: 22.3 us -> 29.3 us  [project(): pl.pallas_call(kernel, name='project', grid_spec=pltpu.PrefetchScalarGrid...]
    pallas_call x3 -> x6, Pallas kernels: 67.4 us -> 68.4 us  [the longest x2 40.2 us: attend(): pl.pallas_call(kernel, name='attend' if leads else 'attend_rest', grid_sp...]
  transfers between devices with their start and end apart: 17 -> 24, of which waited for: 10 -> 9; matrix products, arithmetic and copies ran while one was open for 9% -> 4% of each run, Pallas kernels for 13% -> 15%
where the time goes in v3:
time: 495 us; the launch traced here: 494 us
  waiting for transfers between devices  285 us (58%)
  Pallas kernels  97.7 us (20%)
  starting transfers between devices  87.2 us (18%)
  other arithmetic  14.6 us (3%)
  local copies, waits for them, and re-layouts  8.7 us (2%)
    ppermute x18, waiting for transfers between devices, moved(): return lax.ppermute(cells, 'seq', moves[way])  230 us
    all_to_all x4, waiting for transfers between devices, exchange(): return lax.all_to_all(cells, 'seq', split_axis=0, concat_axis=0, tiled=True)  55 us
    ppermute x18, starting transfers between devices, moved(): return lax.ppermute(cells, 'seq', moves[way])  51.6 us
    pallas_call x2, Pallas kernels, attend(): pl.pallas_call(kernel, name='attend' if leads else 'attend_rest', grid_sp...  40.2 us
    all_to_all x4, starting transfers between devices, exchange(): return lax.all_to_all(cells, 'seq', split_axis=0, concat_axis=0, tiled=True)  35 us
    pallas_call x4, Pallas kernels, project(): pl.pallas_call(kernel, name='project', grid_spec=pltpu.PrefetchScalarGrid...  29.3 us
    pallas_call x1, Pallas kernels, pack(): pl.pallas_call(lead, name='pack', grid=(heads // group,), in_specs=[pl.Bl...  10 us
    pallas_call x2, Pallas kernels, unpack(): pl.pallas_call(kernel, name='unpack' if partial is None else 'unpack_rest...  10 us
  transfers between devices with their start and end apart: 24, of which 9 were waited for; matrix products, arithmetic and copies ran while one was open for 4% of the time, Pallas kernels for 15%

profile of v3, /device:TPU:0, one launch (start us, length us, event | category | flops | bytes accessed | tf_op | source)
XLA Modules:
  0.0 493.9 jit_solution(3246427644366677545)
XLA Ops:
  1.5 10.0 %pack.1 = (bf16[16,800,128]{2,1,0:T(8,128)(2,1)}, s32[16,1,512]{2,1,0:T(1,128)}) custom-call(s32[16,512]{1,0:T(8,128)} %route_ref.1, s32[16,128]{1,0:T(8,128)} %pad.4.pat_ref, bf16[512,2048]{1,0:T(8,128)(2,1)} %q_ref.3, bf16[512,2048]{1,0:T(8,128)(2,1)} %k_ref.3, bf16[512,2048]{1,0:T(8,128)(2,1)} %v_ref.3), custom_call_target="tpu_custom_call" | custom-call | tf_op jit(solution)/shard_map/pack/pallas_call | solution.py:232
  11.5 8.3 %all-to-all-start = ((bf16[16,800,128]{2,1,0:T(8,128)(2,1)}), bf16[16,800,128]{2,1,0:T(8,128)(2,1)S(1)}, u32[]{:S(2)}, u32[]{:S(2)}) async-start(bf16[16,800,128]{2,1,0:T(8,128)(2,1)} %get-tuple-element.12), calls=%async_computation | async-start | bytes 6553600 | tf_op jit(solution)/shard_map/all_to_all | solution.py:544
  19.9 8.2 %pack_rest.1 = bf16[16,768,128]{2,1,0:T(8,128)(2,1)} custom-call(s32[16,1,512]{2,1,0:T(1,128)} %get-tuple-element.11.order_ref, bf16[512,2048]{1,0:T(8,128)(2,1)} %q_ref.3, bf16[512,2048]{1,0:T(8,128)(2,1)} %k_ref.3, bf16[512,2048]{1,0:T(8,128)(2,1)} %v_ref.3), custom_call_target="tpu_custom_call" | custom-call | tf_op jit(solution)/shard_map/pack_rest/pallas_call | solution.py:224
  28.1 55.0 %all-to-all-done.q_ref.k_ref.v_ref = bf16[16,800,128]{2,1,0:T(8,128)(2,1)S(1)} async-done(((bf16[16,800,128]{2,1,0:T(8,128)(2,1)}), bf16[16,800,128]{2,1,0:T(8,128)(2,1)S(1)}, u32[]{:S(2)}, u32[]{:S(2)}) %all-to-all-start) | async-done | bytes 3276832 | tf_op jit(solution)/shard_map/all_to_all | solution.py:544
  83.0 15.8 %all-to-all-start.1 = ((bf16[16,768,128]{2,1,0:T(8,128)(2,1)}), bf16[16,768,128]{2,1,0:T(8,128)(2,1)}, u32[]{:S(2)}, u32[]{:S(2)}) async-start(bf16[16,768,128]{2,1,0:T(8,128)(2,1)} %pack_rest.1), calls=%async_computation.1 | async-start | bytes 6291456 | tf_op jit(solution)/shard_map/all_to_all | solution.py:544
  100.1 4.6 collective-permute-start.2
  104.8 68.6 %collective-permute-done.4 = bf16[2048,256]{1,0:T(8,128)(2,1)S(1)} collective-permute-done((bf16[2048,256]{1,0:T(8,128)(2,1)}, bf16[2048,256]{1,0:T(8,128)(2,1)S(1)}, u32[]{:S(2)}, u32[]{:S(2)}) %collective-permute-start.4) | collective-permute-done | bytes 1048608 | tf_op jit(solution)/shard_map/ppermute | solution.py:493
  174.6 22.0 %collective-permute-start.3 = (bf16[2048,256]{1,0:T(8,128)(2,1)S(1)}, bf16[2048,256]{1,0:T(8,128)(2,1)}, u32[]{:S(2)}, u32[]{:S(2)}) collective-permute-start(bf16[2048,256]{1,0:T(8,128)(2,1)S(1)} %collective-permute-done.2), channel_id=1, source_target_pairs={{0,8},{2,10},{4,12},{6,14},{8,16},{10,18},{12,20},{14,22},{16,24},... | collective-permute-start | bytes 3145736 | tf_op jit(solution)/shard_map/ppermute | solution.py:493
  196.6 19.5 %collective-permute-done.5 = bf16[2048,256]{1,0:T(8,128)(2,1)S(1)} collective-permute-done((bf16[2048,256]{1,0:T(8,128)(2,1)S(1)}, bf16[2048,256]{1,0:T(8,128)(2,1)S(1)}, u32[]{:S(2)}, u32[]{:S(2)}) %collective-permute-start.5) | collective-permute-done | bytes 1048608 | tf_op jit(solution)/shard_map/ppermute | solution.py:493
  218.4 5.6 %collective-permute-start.9 = (bf16[2048,256]{1,0:T(8,128)(2,1)}, bf16[2048,256]{1,0:T(8,128)(2,1)}, u32[]{:S(2)}, u32[]{:S(2)}) collective-permute-start(bf16[2048,256]{1,0:T(8,128)(2,1)} %collective-permute-done.3), channel_id=1, source_target_pairs={{0,8},{2,10},{4,12},{6,14},{8,16},{10,18},{12,20},{14,22},{16,24},... | collective-permute-start | bytes 3145736 | tf_op jit(solution)/shard_map/ppermute | solution.py:493
  224.0 18.6 %collective-permute-done.8 = bf16[2048,256]{1,0:T(8,128)(2,1)S(1)} collective-permute-done((bf16[2048,256]{1,0:T(8,128)(2,1)S(1)}, bf16[2048,256]{1,0:T(8,128)(2,1)S(1)}, u32[]{:S(2)}, u32[]{:S(2)}) %collective-permute-start.8) | collective-permute-done | bytes 1048608 | tf_op jit(solution)/shard_map/ppermute | solution.py:493
  245.5 18.5 %attend.1 = (bf16[16,224,128]{2,1,0:T(8,128)(2,1)}, bf16[512,128]{1,0:T(8,128)(2,1)}, bf16[1024,128]{1,0:T(8,128)(2,1)}, bf16[1024,128]{1,0:T(8,128)(2,1)}) custom-call(s32[320]{0:T(512)} %reshape_squeeze.3.pat_ref, s32[16,512]{1,0:T(8,128)} %reshape.144.slot_ref, bf16[16,800,128]{2,1,0:T(8,128)(2,1)} %copy-done, bf16[16,800,128]{2,1,0:T(8,128)(2,1)} %copy-done, ...), custom_call_target="tpu_custom_call" | custom-call | tf_op jit(solution)/shard_map/attend/pallas_call | solution.py:366
  264.0 5.0 %all-to-all-start.3 = ((bf16[16,224,128]{2,1,0:T(8,128)(2,1)}), bf16[16,224,128]{2,1,0:T(8,128)(2,1)}, u32[]{:S(2)}, u32[]{:S(2)}) async-start(bf16[16,224,128]{2,1,0:T(8,128)(2,1)} %get-tuple-element.16), calls=%async_computation.3 | async-start | bytes 1835008 | tf_op jit(solution)/shard_map/all_to_all | solution.py:544
  271.0 1.9 collective-permute-start.10
  277.1 35.9 %collective-permute-done = bf16[1,1024,256]{2,1,0:T(8,128)(2,1)S(1)} collective-permute-done((bf16[1,1024,256]{2,1,0:T(8,128)(2,1)S(1)}, bf16[1,1024,256]{2,1,0:T(8,128)(2,1)S(1)}, u32[]{:S(2)}, u32[]{:S(2)}) %collective-permute-start) | collective-permute-done | bytes 524320 | tf_op jit(solution)/shard_map/ppermute | solution.py:493
  314.5 2.5 add.141
  318.0 21.7 %attend_rest.1 = bf16[16,288,128]{2,1,0:T(8,128)(2,1)} custom-call(s32[320]{0:T(512)} %reshape_squeeze.3.pat_ref, s32[16,512]{1,0:T(8,128)} %reshape.144.slot_ref, bf16[16,768,128]{2,1,0:T(8,128)(2,1)} %all-to-all-done.1.q_ref.k_ref.v_ref, bf16[16,768,128]{2,1,0:T(8,128)(2,1)} %all-to-all-done.1.q_ref.k_ref.v_ref, ...), custom_call_target="tpu_custom_call" | custom-call | tf_op jit(solution)/shard_map/attend_rest/pallas_call | solution.py:366
  339.7 5.8 %all-to-all-start.2 = ((bf16[16,288,128]{2,1,0:T(8,128)(2,1)}), bf16[16,288,128]{2,1,0:T(8,128)(2,1)}, u32[]{:S(2)}, u32[]{:S(2)}) async-start(bf16[16,288,128]{2,1,0:T(8,128)(2,1)} %attend_rest.1), calls=%async_computation.2 | async-start | bytes 2359296 | tf_op jit(solution)/shard_map/all_to_all | solution.py:544
  345.5 3.1 pad_maximum_fusion.1.refs_10_
  348.7 1.9 collective-permute-start.17
  352.7 2.3 pad_maximum_fusion.5.refs_6_
  355.0 51.2 %collective-permute-done.14 = bf16[1,1024,256]{2,1,0:T(8,128)(2,1)S(1)} collective-permute-done((bf16[1,1024,256]{2,1,0:T(8,128)(2,1)S(1)}, bf16[1,1024,256]{2,1,0:T(8,128)(2,1)S(1)}, u32[]{:S(2)}, u32[]{:S(2)}) %collective-permute-start.14) | collective-permute-done | bytes 524320 | tf_op jit(solution)/shard_map/ppermute | solution.py:493
  408.8 8.4 %collective-permute-done.6 = bf16[1,1024,256]{2,1,0:T(8,128)(2,1)S(1)} collective-permute-done((bf16[1,1024,256]{2,1,0:T(8,128)(2,1)S(1)}, bf16[1,1024,256]{2,1,0:T(8,128)(2,1)S(1)}, u32[]{:S(2)}, u32[]{:S(2)}) %collective-permute-start.6) | collective-permute-done | bytes 524320 | tf_op jit(solution)/shard_map/ppermute | solution.py:493
  417.2 2.4 collective-permute-start.15
  422.9 4.5 unpack.1.refs_0_
  427.4 5.5 %unpack_rest.1.a_ref = bf16[512,2048]{1,0:T(8,128)(2,1)} custom-call(s32[16,1,512]{2,1,0:T(1,128)} %get-tuple-element.11.order_ref, bf16[16,288,128]{2,1,0:T(8,128)(2,1)} %all-to-all-done.2.in_ref, bf16[512,2048]{1,0:T(8,128)(2,1)} %unpack.1.refs_0_), custom_call_target="tpu_custom_call" | custom-call | tf_op jit(solution)/shard_map/unpack_rest/pallas_call | solution.py:399
  433.0 6.8 %collective-permute-done.13.refs_7_ = bf16[2,1024,256]{2,1,0:T(8,128)(2,1)} collective-permute-done((bf16[2,1024,256]{2,1,0:T(8,128)(2,1)}, bf16[2,1024,256]{2,1,0:T(8,128)(2,1)}, u32[]{:S(2)}, u32[]{:S(2)}) %collective-permute-start.13) | collective-permute-done | bytes 1048608 | tf_op jit(solution)/shard_map/ppermute | solution.py:493
  439.8 21.1 %collective-permute-done.15.refs_9_ = bf16[2,1024,256]{2,1,0:T(8,128)(2,1)} collective-permute-done((bf16[2,1024,256]{2,1,0:T(8,128)(2,1)}, bf16[2,1024,256]{2,1,0:T(8,128)(2,1)}, u32[]{:S(2)}, u32[]{:S(2)}) %collective-permute-start.15) | collective-permute-done | bytes 1048608 | tf_op jit(solution)/shard_map/ppermute | solution.py:493
  461.9 7.2 %project.5 = bf16[512,1024]{1,0:T(8,128)(2,1)} custom-call(s32[4,4]{1,0:T(4,128)} %get-tuple-element.25.at_ref, bf16[512,2048]{1,0:T(8,128)(2,1)} %unpack_rest.1.a_ref, bf16[2,1024,256]{2,1,0:T(8,128)(2,1)} %copy-done.2, bf16[2,1024,256]{2,1,0:T(8,128)(2,1)} %collective-permute-done.1.refs_1_, bf16[2,1024,256]{2,1,0:T(8,128)(2,1)} %pad_maximum_fusion.3.refs_2_, ...), custom_call_target="tpu_custom_call" | custom-call | tf_op jit(solution)/shard_map/project/pallas_call | solution.py:463
  469.2 7.2 %project.4 = bf16[512,1024]{1,0:T(8,128)(2,1)} custom-call(s32[4,4]{1,0:T(4,128)} %get-tuple-element.27.at_ref, bf16[512,2048]{1,0:T(8,128)(2,1)} %unpack_rest.1.a_ref, bf16[2,1024,256]{2,1,0:T(8,128)(2,1)} %copy-done.2, bf16[2,1024,256]{2,1,0:T(8,128)(2,1)} %collective-permute-done.1.refs_1_, bf16[2,1024,256]{2,1,0:T(8,128)(2,1)} %pad_maximum_fusion.3.refs_2_, ...), custom_call_target="tpu_custom_call" | custom-call | tf_op jit(solution)/shard_map/project/pallas_call | solution.py:463
  478.0 7.4 %project.6.refs_13_ = bf16[512,2048]{1,0:T(8,128)(2,1)} custom-call(s32[4,4]{1,0:T(4,128)} %get-tuple-element.26.at_ref, bf16[512,2048]{1,0:T(8,128)(2,1)} %unpack_rest.1.a_ref, bf16[2,1024,256]{2,1,0:T(8,128)(2,1)} %copy-done.2, bf16[2,1024,256]{2,1,0:T(8,128)(2,1)} %collective-permute-done.1.refs_1_, bf16[2,1024,256]{2,1,0:T(8,128)(2,1)} %pad_maximum_fusion.3.refs_2_, ...), custom_call_target="tpu_custom_call" | custom-call | tf_op jit(solution)/shard_map/project/pallas_call | solution.py:463
  486.4 7.4 %project.7 = bf16[512,2048]{1,0:T(8,128)(2,1)} custom-call(s32[4,4]{1,0:T(4,128)} %get-tuple-element.28.at_ref, bf16[512,2048]{1,0:T(8,128)(2,1)} %unpack_rest.1.a_ref, bf16[2,1024,256]{2,1,0:T(8,128)(2,1)} %copy-done.2, bf16[2,1024,256]{2,1,0:T(8,128)(2,1)} %collective-permute-done.1.refs_1_, ...), custom_call_target="tpu_custom_call", output_to_operand_aliasing={{}: (15, {})} | custom-call | tf_op jit(solution)/shard_map/project/pallas_call | solution.py:463
  (85 shorter events, 29.3 us)
Async XLA Ops:
  11.5 71.5 %all-to-all-start = ((bf16[16,800,128]{2,1,0:T(8,128)(2,1)}), bf16[16,800,128]{2,1,0:T(8,128)(2,1)S(1)}, u32[]{:S(2)}, u32[]{:S(2)}) async-start(bf16[16,800,128]{2,1,0:T(8,128)(2,1)} %get-tuple-element.12), calls=%async_computation | async-start | bytes 6553600 | tf_op jit(solution)/shard_map/all_to_all | solution.py:544
  83.0 160.8 %copy-start = (bf16[16,800,128]{2,1,0:T(8,128)(2,1)}, bf16[16,800,128]{2,1,0:T(8,128)(2,1)S(1)}, u32[]{:S(2)}) copy-start(bf16[16,800,128]{2,1,0:T(8,128)(2,1)S(1)} %all-to-all-done.q_ref.k_ref.v_ref) | copy-start | bytes 9830404
  83.0 181.0 %all-to-all-start.1 = ((bf16[16,768,128]{2,1,0:T(8,128)(2,1)}), bf16[16,768,128]{2,1,0:T(8,128)(2,1)}, u32[]{:S(2)}, u32[]{:S(2)}) async-start(bf16[16,768,128]{2,1,0:T(8,128)(2,1)} %pack_rest.1), calls=%async_computation.1 | async-start | bytes 6291456 | tf_op jit(solution)/shard_map/all_to_all | solution.py:544
  98.8 74.5 %collective-permute-start.4 = (bf16[2048,256]{1,0:T(8,128)(2,1)}, bf16[2048,256]{1,0:T(8,128)(2,1)S(1)}, u32[]{:S(2)}, u32[]{:S(2)}) collective-permute-start(bf16[2048,256]{1,0:T(8,128)(2,1)} %param.12), channel_id=1, source_target_pairs={{8,0},{10,2},{12,4},{14,6},{16,8},{18,10},{20,12},{22,14},{24,16},... | collective-permute-start | bytes 3145736 | tf_op jit(solution)/shard_map/ppermute | solution.py:493
  100.1 74.5 %collective-permute-start.2 = (bf16[2048,256]{1,0:T(8,128)(2,1)}, bf16[2048,256]{1,0:T(8,128)(2,1)S(1)}, u32[]{:S(2)}, u32[]{:S(2)}) collective-permute-start(bf16[2048,256]{1,0:T(8,128)(2,1)} %param.12), channel_id=1, source_target_pairs={{0,8},{2,10},{4,12},{6,14},{8,16},{10,18},{12,20},{14,22},{16,24},... | collective-permute-start | bytes 3145736 | tf_op jit(solution)/shard_map/ppermute | solution.py:493
  173.3 45.0 %copy-start.10 = (bf16[2048,256]{1,0:T(8,128)(2,1)}, bf16[2048,256]{1,0:T(8,128)(2,1)S(1)}, u32[]{:S(2)}) copy-start(bf16[2048,256]{1,0:T(8,128)(2,1)S(1)} %collective-permute-done.4) | copy-start | bytes 3145732
  173.3 42.8 %collective-permute-start.5 = (bf16[2048,256]{1,0:T(8,128)(2,1)S(1)}, bf16[2048,256]{1,0:T(8,128)(2,1)S(1)}, u32[]{:S(2)}, u32[]{:S(2)}) collective-permute-start(bf16[2048,256]{1,0:T(8,128)(2,1)S(1)} %collective-permute-done.4), channel_id=1, source_target_pairs={{8,0},{10,2},{12,4},{14,6},{16,8},{18,10},{20,12},{22,14},{24,16},... | collective-permute-start | bytes 3145736 | tf_op jit(solution)/shard_map/ppermute | solution.py:493
  174.6 43.7 %collective-permute-start.3 = (bf16[2048,256]{1,0:T(8,128)(2,1)S(1)}, bf16[2048,256]{1,0:T(8,128)(2,1)}, u32[]{:S(2)}, u32[]{:S(2)}) collective-permute-start(bf16[2048,256]{1,0:T(8,128)(2,1)S(1)} %collective-permute-done.2), channel_id=1, source_target_pairs={{0,8},{2,10},{4,12},{6,14},{8,16},{10,18},{12,20},{14,22},{16,24},... | collective-permute-start | bytes 3145736 | tf_op jit(solution)/shard_map/ppermute | solution.py:493
  217.1 25.5 %collective-permute-start.8 = (bf16[2048,256]{1,0:T(8,128)(2,1)S(1)}, bf16[2048,256]{1,0:T(8,128)(2,1)S(1)}, u32[]{:S(2)}, u32[]{:S(2)}) collective-permute-start(bf16[2048,256]{1,0:T(8,128)(2,1)S(1)} %collective-permute-done.5), channel_id=1, source_target_pairs={{8,0},{10,2},{12,4},{14,6},{16,8},{18,10},{20,12},{22,14},{24,16},... | collective-permute-start | bytes 3145736 | tf_op jit(solution)/shard_map/ppermute | solution.py:493
  218.4 50.7 %collective-permute-start.9 = (bf16[2048,256]{1,0:T(8,128)(2,1)}, bf16[2048,256]{1,0:T(8,128)(2,1)}, u32[]{:S(2)}, u32[]{:S(2)}) collective-permute-start(bf16[2048,256]{1,0:T(8,128)(2,1)} %collective-permute-done.3), channel_id=1, source_target_pairs={{0,8},{2,10},{4,12},{6,14},{8,16},{10,18},{12,20},{14,22},{16,24},... | collective-permute-start | bytes 3145736 | tf_op jit(solution)/shard_map/ppermute | solution.py:493
  264.0 5.0 %copy-start.7 = (bf16[2048,256]{1,0:T(8,128)(2,1)S(1)}, bf16[2048,256]{1,0:T(8,128)(2,1)}, u32[]{:S(2)}) copy-start(bf16[2048,256]{1,0:T(8,128)(2,1)} %add.142) | copy-start | bytes 3145732
  264.0 5.1 %copy-start.11 = (bf16[2048,256]{1,0:T(8,128)(2,1)S(1)}, bf16[2048,256]{1,0:T(8,128)(2,1)}, u32[]{:S(2)}) copy-start(bf16[2048,256]{1,0:T(8,128)(2,1)} %copy-done.10) | copy-start | bytes 3145732
  264.0 75.7 %all-to-all-start.3 = ((bf16[16,224,128]{2,1,0:T(8,128)(2,1)}), bf16[16,224,128]{2,1,0:T(8,128)(2,1)}, u32[]{:S(2)}, u32[]{:S(2)}) async-start(bf16[16,224,128]{2,1,0:T(8,128)(2,1)} %get-tuple-element.16), calls=%async_computation.3 | async-start | bytes 1835008 | tf_op jit(solution)/shard_map/all_to_all | solution.py:544
  270.9 4.6 copy-start.14
  271.0 46.0 %collective-permute-start.10 = (bf16[2,1024,256]{2,1,0:T(8,128)(2,1)S(1)}, bf16[2,1024,256]{2,1,0:T(8,128)(2,1)S(1)}, u32[]{:S(2)}, u32[]{:S(2)}) collective-permute-start(bf16[2,1024,256]{2,1,0:T(8,128)(2,1)S(1)} %pad_maximum_fusion.4), channel_id=1, source_target_pairs={{0,4},{2,6},{4,0},{6,2},{8,12},{10,14},{12,8},{14,10},{16,20},{18,... | collective-permute-start | bytes 3145736 | tf_op jit(solution)/shard_map/ppermute | solution.py:493
  274.0 40.5 %copy-start.9 = (bf16[2048,256]{1,0:T(8,128)(2,1)S(1)}, bf16[2048,256]{1,0:T(8,128)(2,1)}, u32[]{:S(2)}) copy-start(bf16[2048,256]{1,0:T(8,128)(2,1)} %copy-done.8) | copy-start | bytes 3145732
  274.0 71.5 %collective-permute-start.16 = (bf16[2,1024,256]{2,1,0:T(8,128)(2,1)}, bf16[2,1024,256]{2,1,0:T(8,128)(2,1)}, u32[]{:S(2)}, u32[]{:S(2)}) collective-permute-start(bf16[2,1024,256]{2,1,0:T(8,128)(2,1)} %pad_maximum_fusion.7), channel_id=1, source_target_pairs={{0,2},{2,0},{4,6},{6,4},{8,10},{10,8},{12,14},{14,12},{16,18},{18,... | collective-permute-start | bytes 3145736 | tf_op jit(solution)/shard_map/ppermute | solution.py:493
  276.4 36.6 %collective-permute-start = (bf16[1,1024,256]{2,1,0:T(8,128)(2,1)S(1)}, bf16[1,1024,256]{2,1,0:T(8,128)(2,1)S(1)}, u32[]{:S(2)}, u32[]{:S(2)}) collective-permute-start(bf16[1,1024,256]{2,1,0:T(8,128)(2,1)S(1)} %get-tuple-element.24), channel_id=1, source_target_pairs={{0,4},{2,6},{4,0},{6,2},{8,12},{10,14},{12,8},{14,10},{16,20},{18,... | collective-permute-start | bytes 1572872 | tf_op jit(solution)/shard_map/ppermute | solution.py:493
  276.9 75.2 %collective-permute-start.12 = (bf16[1,1024,256]{2,1,0:T(8,128)(2,1)}, bf16[1,1024,256]{2,1,0:T(8,128)(2,1)}, u32[]{:S(2)}, u32[]{:S(2)}) collective-permute-start(bf16[1,1024,256]{2,1,0:T(8,128)(2,1)} %get-tuple-element.23), channel_id=1, source_target_pairs={{0,2},{2,0},{4,6},{6,4},{8,10},{10,8},{12,14},{14,12},{16,18},{18,... | collective-permute-start | bytes 1572872 | tf_op jit(solution)/shard_map/ppermute | solution.py:493
  313.1 107.6 %collective-permute-start.1 = (bf16[2,1024,256]{2,1,0:T(8,128)(2,1)S(1)}, bf16[2,1024,256]{2,1,0:T(8,128)(2,1)}, u32[]{:S(2)}, u32[]{:S(2)}) collective-permute-start(bf16[2,1024,256]{2,1,0:T(8,128)(2,1)S(1)} %pad_maximum_fusion.2.refs_0_), channel_id=1, source_target_pairs={{0,2},{2,0},{4,6},{6,4},{8,10},{10,8},{12,14},{14,12},{16,18},{18,... | collective-permute-start | bytes 3145736 | tf_op jit(solution)/shard_map/ppermute | solution.py:493
  317.2 22.5 %copy-start.1 = (bf16[4,1024,256]{2,1,0:T(8,128)(2,1)}, bf16[4,1024,256]{2,1,0:T(8,128)(2,1)S(1)}, u32[]{:S(2)}) copy-start(bf16[4,1024,256]{2,1,0:T(8,128)(2,1)S(1)} %pad_maximum_fusion.refs_4_) | copy-start | bytes 6291460
  317.2 143.7 %collective-permute-start.11 = (bf16[4,1024,256]{2,1,0:T(8,128)(2,1)S(1)}, bf16[4,1024,256]{2,1,0:T(8,128)(2,1)}, u32[]{:S(2)}, u32[]{:S(2)}) collective-permute-start(bf16[4,1024,256]{2,1,0:T(8,128)(2,1)S(1)} %pad_maximum_fusion.refs_4_), channel_id=1, source_target_pairs={{0,2},{2,0},{4,6},{6,4},{8,10},{10,8},{12,14},{14,12},{16,18},{18,... | collective-permute-start | bytes 6291464 | tf_op jit(solution)/shard_map/ppermute | solution.py:493
  339.7 87.7 %all-to-all-start.2 = ((bf16[16,288,128]{2,1,0:T(8,128)(2,1)}), bf16[16,288,128]{2,1,0:T(8,128)(2,1)}, u32[]{:S(2)}, u32[]{:S(2)}) async-start(bf16[16,288,128]{2,1,0:T(8,128)(2,1)} %attend_rest.1), calls=%async_computation.2 | async-start | bytes 2359296 | tf_op jit(solution)/shard_map/all_to_all | solution.py:544
  345.5 5.0 %copy-start.6 = (bf16[2048,256]{1,0:T(8,128)(2,1)S(1)}, bf16[2048,256]{1,0:T(8,128)(2,1)}, u32[]{:S(2)}) copy-start(bf16[2048,256]{1,0:T(8,128)(2,1)} %add.141) | copy-start | bytes 3145732
  348.7 112.2 %collective-permute-start.17 = (bf16[4,1024,256]{2,1,0:T(8,128)(2,1)}, bf16[4,1024,256]{2,1,0:T(8,128)(2,1)}, u32[]{:S(2)}, u32[]{:S(2)}) collective-permute-start(bf16[4,1024,256]{2,1,0:T(8,128)(2,1)} %pad_maximum_fusion.1.refs_10_), channel_id=1, source_target_pairs={{0,4},{2,6},{4,0},{6,2},{8,12},{10,14},{12,8},{14,10},{16,20},{18,... | collective-permute-start | bytes 6291464 | tf_op jit(solution)/shard_map/ppermute | solution.py:493
  350.6 55.6 %collective-permute-start.14 = (bf16[1,1024,256]{2,1,0:T(8,128)(2,1)S(1)}, bf16[1,1024,256]{2,1,0:T(8,128)(2,1)S(1)}, u32[]{:S(2)}, u32[]{:S(2)}) collective-permute-start(bf16[1,1024,256]{2,1,0:T(8,128)(2,1)S(1)} %get-tuple-element.21), channel_id=1, source_target_pairs={{0,2},{2,0},{4,6},{6,4},{8,10},{10,8},{12,14},{14,12},{16,18},{18,... | collective-permute-start | bytes 1572872 | tf_op jit(solution)/shard_map/ppermute | solution.py:493
  352.1 65.1 %collective-permute-start.6 = (bf16[1,1024,256]{2,1,0:T(8,128)(2,1)S(1)}, bf16[1,1024,256]{2,1,0:T(8,128)(2,1)S(1)}, u32[]{:S(2)}, u32[]{:S(2)}) collective-permute-start(bf16[1,1024,256]{2,1,0:T(8,128)(2,1)S(1)} %get-tuple-element.22), channel_id=1, source_target_pairs={{0,4},{2,6},{4,0},{6,2},{8,12},{10,14},{12,8},{14,10},{16,20},{18,... | collective-permute-start | bytes 1572872 | tf_op jit(solution)/shard_map/ppermute | solution.py:493
  406.2 33.6 %collective-permute-start.13 = (bf16[2,1024,256]{2,1,0:T(8,128)(2,1)}, bf16[2,1024,256]{2,1,0:T(8,128)(2,1)}, u32[]{:S(2)}, u32[]{:S(2)}) collective-permute-start(bf16[2,1024,256]{2,1,0:T(8,128)(2,1)} %pad_maximum_fusion.5.refs_6_), channel_id=1, source_target_pairs={{0,4},{2,6},{4,0},{6,2},{8,12},{10,14},{12,8},{14,10},{16,20},{18,... | collective-permute-start | bytes 3145736 | tf_op jit(solution)/shard_map/ppermute | solution.py:493
  417.2 43.7 %collective-permute-start.15 = (bf16[2,1024,256]{2,1,0:T(8,128)(2,1)}, bf16[2,1024,256]{2,1,0:T(8,128)(2,1)}, u32[]{:S(2)}, u32[]{:S(2)}) collective-permute-start(bf16[2,1024,256]{2,1,0:T(8,128)(2,1)} %pad_maximum_fusion.6.refs_8_), channel_id=1, source_target_pairs={{0,4},{2,6},{4,0},{6,2},{8,12},{10,14},{12,8},{14,10},{16,20},{18,... | collective-permute-start | bytes 3145736 | tf_op jit(solution)/shard_map/ppermute | solution.py:493
  420.7 40.2 %collective-permute-start.7 = (bf16[2,1024,256]{2,1,0:T(8,128)(2,1)}, bf16[2,1024,256]{2,1,0:T(8,128)(2,1)S(1)}, u32[]{:S(2)}, u32[]{:S(2)}) collective-permute-start(bf16[2,1024,256]{2,1,0:T(8,128)(2,1)} %pad_maximum_fusion.3.refs_2_), channel_id=1, source_target_pairs={{0,2},{2,0},{4,6},{6,4},{8,10},{10,8},{12,14},{14,12},{16,18},{18,... | collective-permute-start | bytes 3145736 | tf_op jit(solution)/shard_map/ppermute | solution.py:493
  469.1 7.9 %collective-permute-start.19 = (bf16[512,1024]{1,0:T(8,128)(2,1)}, bf16[512,1024]{1,0:T(8,128)(2,1)S(1)}, u32[]{:S(2)}, u32[]{:S(2)}) collective-permute-start(bf16[512,1024]{1,0:T(8,128)(2,1)} %project.5), channel_id=1, source_target_pairs={{0,1},{1,0},{2,3},{3,2},{4,5},{5,4},{6,7},{7,6},{8,9},{9,8},{10,11... | collective-permute-start | bytes 3145736 | tf_op jit(solution)/shard_map/ppermute | solution.py:567
  476.4 8.9 %collective-permute-start.18 = (bf16[512,1024]{1,0:T(8,128)(2,1)}, bf16[512,1024]{1,0:T(8,128)(2,1)S(1)}, u32[]{:S(2)}, u32[]{:S(2)}) collective-permute-start(bf16[512,1024]{1,0:T(8,128)(2,1)} %project.4), channel_id=1, source_target_pairs={{0,1},{1,0},{2,3},{3,2},{4,5},{5,4},{6,7},{7,6},{8,9},{9,8},{10,11... | collective-permute-start | bytes 3145736 | tf_op jit(solution)/shard_map/ppermute | solution.py:567
  (7 other events, 15.0 us)
